TPU v7x, 32 devices: a whole 2x2x4 slice. The times are simulated.
32 devices in a mesh: ctx: 16 (over z, x, core), chan: 2 (over y).
Axes of the slice: x: 2, y: 2, z: 4, core: 2. Of those that a mesh axis runs over, the one named last changes fastest.
Arguments:
- gated_input: bfloat16 [4096, 8192], P('ctx', 'chan'), may hold values from -6 to 6
- query: bfloat16 [4096, 8192], P('ctx', 'chan'), may hold values from -6 to 6
- out_grad: bfloat16 [4096, 8192], P('ctx', 'chan'), may hold values from -6 to 6
- out_weight: bfloat16 [8192, 8192], P('chan', 'ctx'), may hold values from -0.0625 to 0.0625
- decay_rate: float32 [16, 8192], P(None, 'chan'), may hold values from 2.4414063e-05 to 0.083333333
- residue: float32 [16, 8192], P(None, 'chan'), may hold values from -0.5 to 0.5
Outputs:
- grad_query: bfloat16 [4096, 8192], P('ctx', 'chan')
- grad_input: bfloat16 [4096, 8192], P('ctx', 'chan')
All inputs are finite; a program needn't handle non-finite values.
Results may differ from a plain program's by a relative error of at most 0.0013.
Values may be sent and summed in bfloat16 or wider, within the bound.
A program may use at most 576 MiB of HBM per device.

v0:
```python
import jax
import jax.numpy as jnp
import numpy as np
from jax import lax
from jax.sharding import PartitionSpec as P

block_rows = 64
full_precision = lax.Precision.HIGHEST


def passed_along(value, axis, steps):
    count = lax.axis_size(axis)
    initial, last = (max(0, -steps), min(count, count - steps))
    return lax.ppermute(value, axis, [(source, source + steps) for source in range(initial, last)])


def on_device(gated_input, query, out_grad, out_weight, decay_rate, residue):
    tok_rows, chan_width = gated_input.shape
    block_count = tok_rows // block_rows
    lag_steps = jnp.arange(block_rows, dtype=jnp.float32)
    filter_taps = jnp.sum(
        residue[None] * jnp.exp(-decay_rate[None] * lag_steps[:, None, None]), axis=1
    )
    lag_offsets = np.arange(block_rows)[:, None] - np.arange(block_rows)[None, :]
    lag_table = np.where(lag_offsets >= 0, lag_offsets, block_rows).reshape(-1).astype(np.int32)
    padded_taps = jnp.concatenate([filter_taps, jnp.zeros((1, chan_width), jnp.float32)], axis=0)
    toeplitz = jnp.take(padded_taps, jnp.asarray(lag_table), axis=0).reshape(
        block_rows, block_rows, chan_width
    )
    to_end = jnp.exp(-decay_rate[None] * (block_rows - 1.0 - lag_steps)[:, None, None])
    from_start = jnp.exp(-decay_rate[None] * lag_steps[:, None, None])
    into_rows = residue[None] * jnp.exp(-decay_rate[None] * (lag_steps + 1.0)[:, None, None])
    back_rows = residue[None] * jnp.exp(-decay_rate[None] * (block_rows - lag_steps)[:, None, None])
    block_index = jnp.arange(block_count, dtype=jnp.float32)
    state_index = jnp.arange(block_count + 1, dtype=jnp.float32)
    gap_blocks = state_index[:, None] - 1.0 - block_index[None, :]
    fwd_coef = jnp.where(
        (gap_blocks >= 0.0)[:, :, None, None],
        jnp.exp(
            -decay_rate[None, None] * block_rows * jnp.maximum(gap_blocks, 0.0)[:, :, None, None]
        ),
        0.0,
    )
    back_coef = fwd_coef[::-1, ::-1]
    chain_decay = jnp.exp(-decay_rate * tok_rows)
    zero_state = jnp.zeros_like(chain_decay)
    input_blocks = gated_input.astype(jnp.float32).reshape(block_count, block_rows, chan_width)
    local_part = jnp.einsum("tsc,nsc->ntc", toeplitz, input_blocks, precision=full_precision)
    block_ends = jnp.einsum("smc,nsc->nmc", to_end, input_blocks, precision=full_precision)
    block_states = jnp.einsum("nkmc,kmc->nmc", fwd_coef, block_ends, precision=full_precision)
    local_end = block_states[block_count]

    def relay_forward(hop_index, state_pair):
        arrived = passed_along(state_pair[1], "ctx", 1)
        return (arrived, chain_decay * arrived + local_end)

    earlier_state = lax.fori_loop(
        0, lax.axis_size("ctx") - 1, relay_forward, (zero_state, local_end)
    )[0]
    start_states = (
        block_states[:block_count]
        + jnp.exp(-decay_rate[None] * block_rows * block_index[:, None, None]) * earlier_state[None]
    )
    carried = jnp.einsum("tmc,nmc->ntc", into_rows, start_states, precision=full_precision)
    conv_out = (local_part + carried).reshape(tok_rows, chan_width)
    grad_rows = lax.all_gather(out_grad, "chan", axis=1, tiled=True)
    grad_mixed = lax.dot_general(
        grad_rows,
        lax.all_gather(out_weight, "ctx", axis=1, tiled=True),
        (((1,), (1,)), ((), ())),
        preferred_element_type=jnp.float32,
    )
    grad_query = (grad_mixed * conv_out).astype(jnp.bfloat16)
    grad_conv = (grad_mixed * query.astype(jnp.float32)).reshape(
        block_count, block_rows, chan_width
    )
    local_back = jnp.einsum("tsc,ntc->nsc", toeplitz, grad_conv, precision=full_precision)
    block_heads = jnp.einsum("tmc,ntc->nmc", from_start, grad_conv, precision=full_precision)
    block_tails = jnp.einsum("nkmc,kmc->nmc", back_coef, block_heads, precision=full_precision)
    local_out = block_tails[0]

    def relay_backward(hop_index, state_pair):
        arrived = passed_along(state_pair[1], "ctx", -1)
        return (arrived, chain_decay * arrived + local_out)

    later_state = lax.fori_loop(
        0, lax.axis_size("ctx") - 1, relay_backward, (zero_state, local_out)
    )[0]
    end_states = (
        block_tails[1:]
        + jnp.exp(-decay_rate[None] * block_rows * (block_count - 1.0 - block_index)[:, None, None])
        * later_state[None]
    )
    carried_back = jnp.einsum("smc,nmc->nsc", back_rows, end_states, precision=full_precision)
    grad_input = (local_back + carried_back).reshape(tok_rows, chan_width).astype(jnp.bfloat16)
    return (grad_query, grad_input)


def solution(mesh):
    return jax.shard_map(
        on_device,
        mesh=mesh,
        in_specs=(
            P("ctx", "chan"),
            P("ctx", "chan"),
            P("ctx", "chan"),
            P("chan", "ctx"),
            P(None, "chan"),
            P(None, "chan"),
        ),
        out_specs=(P("ctx", "chan"), P("ctx", "chan")),
        check_vma=False,
    )
```

profile of v0, /device:TPU:23, one launch (start us, length us, event | category | flops | bytes accessed | tf_op | source)
XLA Modules:
  0.0 1066.5 jit_solution(10012313281182289095)
XLA Ops:
  15.4 34.6 %fusion.24 = f32[16,4096,4]{0,2,1:T(4,128)} fusion(bf16[4,64,4096]{1,0,2:T(4,128)(2,1)} %copy.33, f32[64]{0:T(128)S(1)} %iota_subtract_fusion.3, f32[16,4096]{0,1:T(8,128)} %copy.30), kind=kOutput, calls=%fused_computation.29 | convolution fusion | flops 205520896 | bytes 3408128 | tf_op jit(solution)/shard_map/smc,nsc->nmc/dot_general | solution.py:49
  58.8 212.4 %while.24 = (s32[]{:T(128)}, f32[16,4096]{1,0:T(8,128)}, f32[16,4096]{1,0:T(8,128)S(1)}, f32[16,4096]{1,0:T(8,128)S(1)}, f32[16,4096]{1,0:T(8,128)S(1)}, /*index=5*/s32[]{:T(128)}) while((s32[]{:T(128)}, f32[16,4096]{1,0:T(8,128)}, f32[16,4096]{1,0:T(8,128)S(1)}, f32[16,4096]{1,0:T(8,128)S(1)}, f32[16,4096]{1,0:T(8,128)S(1)}, ...), condition=%wide.region_2.3_spmd, body=%wide.region_1.2_spmd.sunk | while | flops 131074 | bytes 3145865 | solution.py:57
  96.1 9.0 collective-permute-done
  111.2 9.0 collective-permute-done
  126.2 9.0 collective-permute-done
  141.2 9.0 collective-permute-done
  156.2 9.0 collective-permute-done
  171.3 9.0 collective-permute-done
  186.3 9.0 collective-permute-done
  201.3 9.0 collective-permute-done
  216.3 9.0 collective-permute-done
  231.4 9.0 collective-permute-done
  246.4 9.0 collective-permute-done
  261.4 9.0 collective-permute-done
  281.2 26.0 %multiply_reduce_fusion = f32[64,4096]{0,1:T(8,128)} fusion(f32[16,4096]{0,1:T(8,128)S(1)} %copy-done.7, f32[16,4096]{0,1:T(8,128)} %copy.29), kind=kLoop, calls=%fused_computation.14 | loop fusion | flops 12320768 | bytes 1572864 | tf_op jit(solution)/shard_map/reduce_sum | solution.py:21
  309.6 33.3 %gather_fusion = f32[4096,4096]{1,0:T(8,128)} fusion(f32[65,4096]{1,0:T(8,128)S(1)} %concatenate.3, s32[4096]{0:T(1024)S(1)} %broadcast_clamp_fusion), kind=kCustom, calls=%fused_computation | custom fusion | bytes 134234112 | tf_op jit(solution)/shard_map/jit(_take)/gather | solution.py:27
  342.8 116.0 %copy.32 = f32[64,64,4096]{1,0,2:T(8,128)} copy(f32[64,64,4096]{2,1,0:T(8,128)} %bitcast.4) | data formatting | bytes 134217728 | tf_op jit(solution)/shard_map/jit(_take)/gather | solution.py:27
  458.9 46.7 %fusion.4 = f32[4096,4,64]{2,1,0:T(4,128)} fusion(f32[4,16,4096]{1,0,2:T(4,128)} %copy.35, f32[64]{0:T(128)S(1)} %iota_add_fusion, f32[16,4096]{0,1:T(8,128)S(1)} %copy-done.8, f32[16,4096]{0,1:T(8,128)} %copy.29), kind=kOutput, calls=%fused_computation.7 | convolution fusion | flops 209715200 | bytes 5767424 | tf_op jit(solution)/shard_map/tmc,nmc->ntc/dot_general | solution.py:64
  505.6 110.8 %bitcast_add_fusion = f32[4,64,4096]{1,0,2:T(4,128)} fusion(f32[4096,4,64]{2,1,0:T(4,128)} %fusion.4, f32[64,64,4096]{1,0,2:T(8,128)} %copy.32, bf16[4,64,4096]{1,0,2:T(4,128)(2,1)} %copy.33), kind=kOutput, calls=%fused_computation.26 | convolution fusion | flops 806354944 | bytes 77594624 | tf_op jit(solution)/shard_map/tsc,nsc->ntc/dot_general | solution.py:48
  628.3 32.8 %convert_multiply_fusion = (f32[256,4096]{1,0:T(8,128)}, bf16[256,4096]{1,0:T(8,128)(2,1)}) fusion(bf16[256,4096]{1,0:T(8,128)(2,1)} %param.12, f32[4,64,4096]{2,1,0:T(8,128)} %copy.36, bf16[256,8192]{1,0:T(8,128)(2,1)} %all-gather.3.cloned.1.call-done, bf16[4096,8192]{1,0:T(8,128)(2,1)} %all-gather.5.cloned.1.call-done), kind=kOutput, calls=%fused_computation.35 | convolution fusion | flops 17184063488 | bytes 83886080 | tf_op jit(solution)/shard_map/dot_general | solution.py:67
  669.6 58.2 %fusion.23 = f32[16,4096,4]{0,2,1:T(4,128)} fusion(f32[4,64,4096]{1,0,2:T(4,128)} %copy.37, f32[16,4096]{0,1:T(8,128)S(1)} %copy-done.8), kind=kOutput, calls=%fused_computation.28 | convolution fusion | flops 205520896 | bytes 5505024 | tf_op jit(solution)/shard_map/tmc,ntc->nmc/dot_general | solution.py:78
  727.8 119.6 %fusion.33 = f32[4096,4,64]{2,1,0:T(4,128)} fusion(f32[4,64,4096]{1,0,2:T(4,128)} %copy.37, f32[64,64,4096]{1,0,2:T(8,128)} %copy.32), kind=kOutput, calls=%fused_computation.52 | convolution fusion | flops 805306368 | bytes 75497472 | tf_op jit(solution)/shard_map/tsc,ntc->nsc/dot_general | solution.py:77
  858.1 140.0 %while.25 = (s32[]{:T(128)}, f32[16,4096]{1,0:T(8,128)}, f32[16,4096]{1,0:T(8,128)S(1)}, f32[16,4096]{1,0:T(8,128)S(1)}, f32[16,4096]{1,0:T(8,128)S(1)}, /*index=5*/s32[]{:T(128)}) while((s32[]{:T(128)}, f32[16,4096]{1,0:T(8,128)}, f32[16,4096]{1,0:T(8,128)S(1)}, f32[16,4096]{1,0:T(8,128)S(1)}, f32[16,4096]{1,0:T(8,128)S(1)}, ...), condition=%wide.region_4.5_spmd, body=%wide.region_3.4_spmd.sunk | while | flops 131074 | bytes 3145865 | solution.py:86
  1005.2 47.3 %fusion.28 = bf16[4,64,4096]{1,0,2:T(4,128)(2,1)} fusion(f32[4096,4,64]{2,1,0:T(4,128)} %fusion.33, f32[4,16,4096]{1,0,2:T(4,128)} %copy.40, f32[64]{0:T(128)S(1)} %iota_subtract_fusion.1, f32[16,4096]{0,1:T(8,128)S(1)} %copy-done.9, f32[16,4096]{0,1:T(8,128)} %copy.29), kind=kOutput, calls=%fused_computation.36 | convolution fusion | flops 211812352 | bytes 7864576 | tf_op jit(solution)/shard_map/smc,nmc->nsc/dot_general | solution.py:94
  (204 shorter events, 317.9 us)
Async XLA Ops:
  7.2 621.2 %all-gather.3.cloned.1.call-start = ((), (), s32[]{:S(2)}) async-start(), calls=%async_computation | async-start | bytes 6291456 | tf_op jit(solution)/shard_map/all_gather | solution.py:66
  7.9 620.4 %all-gather.5.cloned.1.call-start = ((), (), s32[]{:S(2)}) async-start(), calls=%async_computation.1 | async-start | bytes 71303168 | tf_op jit(solution)/shard_map/all_gather | solution.py:69
  66.5 8.6 collective-permute-start
  75.8 14.3 %collective-permute-start = (f32[16,4096]{1,0:T(8,128)S(1)}, f32[16,4096]{1,0:T(8,128)S(1)}, u32[]{:S(2)}, u32[]{:S(2)}) collective-permute-start(f32[16,4096]{1,0:T(8,128)S(1)} %get-tuple-element.149), channel_id=1, source_target_pairs={{0,2},{2,4},{4,6},{6,8},{8,10},{10,12},{12,14},{14,16},{16,18},{18... | collective-permute-start | bytes 786440 | tf_op jit(solution)/shard_map/while/body/eval_jaxpr/ppermute | solution.py:14
  90.8 14.3 %collective-permute-start = (f32[16,4096]{1,0:T(8,128)S(1)}, f32[16,4096]{1,0:T(8,128)S(1)}, u32[]{:S(2)}, u32[]{:S(2)}) collective-permute-start(f32[16,4096]{1,0:T(8,128)S(1)} %get-tuple-element.149), channel_id=1, source_target_pairs={{0,2},{2,4},{4,6},{6,8},{8,10},{10,12},{12,14},{14,16},{16,18},{18... | collective-permute-start | bytes 786440 | tf_op jit(solution)/shard_map/while/body/eval_jaxpr/ppermute | solution.py:14
  105.9 14.3 %collective-permute-start = (f32[16,4096]{1,0:T(8,128)S(1)}, f32[16,4096]{1,0:T(8,128)S(1)}, u32[]{:S(2)}, u32[]{:S(2)}) collective-permute-start(f32[16,4096]{1,0:T(8,128)S(1)} %get-tuple-element.149), channel_id=1, source_target_pairs={{0,2},{2,4},{4,6},{6,8},{8,10},{10,12},{12,14},{14,16},{16,18},{18... | collective-permute-start | bytes 786440 | tf_op jit(solution)/shard_map/while/body/eval_jaxpr/ppermute | solution.py:14
  120.9 14.3 %collective-permute-start = (f32[16,4096]{1,0:T(8,128)S(1)}, f32[16,4096]{1,0:T(8,128)S(1)}, u32[]{:S(2)}, u32[]{:S(2)}) collective-permute-start(f32[16,4096]{1,0:T(8,128)S(1)} %get-tuple-element.149), channel_id=1, source_target_pairs={{0,2},{2,4},{4,6},{6,8},{8,10},{10,12},{12,14},{14,16},{16,18},{18... | collective-permute-start | bytes 786440 | tf_op jit(solution)/shard_map/while/body/eval_jaxpr/ppermute | solution.py:14
  135.9 14.3 %collective-permute-start = (f32[16,4096]{1,0:T(8,128)S(1)}, f32[16,4096]{1,0:T(8,128)S(1)}, u32[]{:S(2)}, u32[]{:S(2)}) collective-permute-start(f32[16,4096]{1,0:T(8,128)S(1)} %get-tuple-element.149), channel_id=1, source_target_pairs={{0,2},{2,4},{4,6},{6,8},{8,10},{10,12},{12,14},{14,16},{16,18},{18... | collective-permute-start | bytes 786440 | tf_op jit(solution)/shard_map/while/body/eval_jaxpr/ppermute | solution.py:14
  151.0 14.3 %collective-permute-start = (f32[16,4096]{1,0:T(8,128)S(1)}, f32[16,4096]{1,0:T(8,128)S(1)}, u32[]{:S(2)}, u32[]{:S(2)}) collective-permute-start(f32[16,4096]{1,0:T(8,128)S(1)} %get-tuple-element.149), channel_id=1, source_target_pairs={{0,2},{2,4},{4,6},{6,8},{8,10},{10,12},{12,14},{14,16},{16,18},{18... | collective-permute-start | bytes 786440 | tf_op jit(solution)/shard_map/while/body/eval_jaxpr/ppermute | solution.py:14
  166.0 14.3 %collective-permute-start = (f32[16,4096]{1,0:T(8,128)S(1)}, f32[16,4096]{1,0:T(8,128)S(1)}, u32[]{:S(2)}, u32[]{:S(2)}) collective-permute-start(f32[16,4096]{1,0:T(8,128)S(1)} %get-tuple-element.149), channel_id=1, source_target_pairs={{0,2},{2,4},{4,6},{6,8},{8,10},{10,12},{12,14},{14,16},{16,18},{18... | collective-permute-start | bytes 786440 | tf_op jit(solution)/shard_map/while/body/eval_jaxpr/ppermute | solution.py:14
  181.0 14.3 %collective-permute-start = (f32[16,4096]{1,0:T(8,128)S(1)}, f32[16,4096]{1,0:T(8,128)S(1)}, u32[]{:S(2)}, u32[]{:S(2)}) collective-permute-start(f32[16,4096]{1,0:T(8,128)S(1)} %get-tuple-element.149), channel_id=1, source_target_pairs={{0,2},{2,4},{4,6},{6,8},{8,10},{10,12},{12,14},{14,16},{16,18},{18... | collective-permute-start | bytes 786440 | tf_op jit(solution)/shard_map/while/body/eval_jaxpr/ppermute | solution.py:14
  196.0 14.3 %collective-permute-start = (f32[16,4096]{1,0:T(8,128)S(1)}, f32[16,4096]{1,0:T(8,128)S(1)}, u32[]{:S(2)}, u32[]{:S(2)}) collective-permute-start(f32[16,4096]{1,0:T(8,128)S(1)} %get-tuple-element.149), channel_id=1, source_target_pairs={{0,2},{2,4},{4,6},{6,8},{8,10},{10,12},{12,14},{14,16},{16,18},{18... | collective-permute-start | bytes 786440 | tf_op jit(solution)/shard_map/while/body/eval_jaxpr/ppermute | solution.py:14
  211.1 14.3 %collective-permute-start = (f32[16,4096]{1,0:T(8,128)S(1)}, f32[16,4096]{1,0:T(8,128)S(1)}, u32[]{:S(2)}, u32[]{:S(2)}) collective-permute-start(f32[16,4096]{1,0:T(8,128)S(1)} %get-tuple-element.149), channel_id=1, source_target_pairs={{0,2},{2,4},{4,6},{6,8},{8,10},{10,12},{12,14},{14,16},{16,18},{18... | collective-permute-start | bytes 786440 | tf_op jit(solution)/shard_map/while/body/eval_jaxpr/ppermute | solution.py:14
  226.1 14.3 %collective-permute-start = (f32[16,4096]{1,0:T(8,128)S(1)}, f32[16,4096]{1,0:T(8,128)S(1)}, u32[]{:S(2)}, u32[]{:S(2)}) collective-permute-start(f32[16,4096]{1,0:T(8,128)S(1)} %get-tuple-element.149), channel_id=1, source_target_pairs={{0,2},{2,4},{4,6},{6,8},{8,10},{10,12},{12,14},{14,16},{16,18},{18... | collective-permute-start | bytes 786440 | tf_op jit(solution)/shard_map/while/body/eval_jaxpr/ppermute | solution.py:14
  241.1 14.3 %collective-permute-start = (f32[16,4096]{1,0:T(8,128)S(1)}, f32[16,4096]{1,0:T(8,128)S(1)}, u32[]{:S(2)}, u32[]{:S(2)}) collective-permute-start(f32[16,4096]{1,0:T(8,128)S(1)} %get-tuple-element.149), channel_id=1, source_target_pairs={{0,2},{2,4},{4,6},{6,8},{8,10},{10,12},{12,14},{14,16},{16,18},{18... | collective-permute-start | bytes 786440 | tf_op jit(solution)/shard_map/while/body/eval_jaxpr/ppermute | solution.py:14
  256.1 14.3 %collective-permute-start = (f32[16,4096]{1,0:T(8,128)S(1)}, f32[16,4096]{1,0:T(8,128)S(1)}, u32[]{:S(2)}, u32[]{:S(2)}) collective-permute-start(f32[16,4096]{1,0:T(8,128)S(1)} %get-tuple-element.149), channel_id=1, source_target_pairs={{0,2},{2,4},{4,6},{6,8},{8,10},{10,12},{12,14},{14,16},{16,18},{18... | collective-permute-start | bytes 786440 | tf_op jit(solution)/shard_map/while/body/eval_jaxpr/ppermute | solution.py:14
  858.1 9.3 collective-permute-start.1
  868.2 8.6 collective-permute-start.1
  877.5 8.6 collective-permute-start.1
  886.7 8.6 collective-permute-start.1
  905.3 8.6 collective-permute-start.1
  914.6 8.6 collective-permute-start.1
  933.1 8.6 collective-permute-start.1
  942.4 8.6 collective-permute-start.1
  (52 other events, 554.5 us)
Sparse Core Ops, SparseCore 0:
  9.5 56.6 all-gather.2
  67.8 363.1 all-gather.4
where the time goes:
time: 1080 us; the launch traced here: 1070 us
  matrix products  450 us (42%)
  local copies, waits for them, and re-layouts  232 us (21%)
  waiting for transfers between devices  226 us (21%)
  starting transfers between devices  106 us (10%)
  other arithmetic  37.4 us (3%)
  between operations  14.5 us (1%)
    ppermute x30, waiting for transfers between devices, passed_along(): lax.ppermute(value, axis, [(source, source + steps) for source in range(i...  225 us
    gather x2, local copies, waits for them, and re-layouts, on_device(): jnp.take(padded_taps, jnp.asarray(lag_table), axis=0)  149 us
    dot_general x1, matrix products, on_device(): jnp.einsum('tsc,ntc->nsc', toeplitz, grad_conv, precision=full_precision)  120 us
    dot_general x1, matrix products, on_device(): jnp.einsum('tsc,nsc->ntc', toeplitz, input_blocks, precision=full_precision)  111 us
    ppermute x30, starting transfers between devices, passed_along(): lax.ppermute(value, axis, [(source, source + steps) for source in range(i...  106 us
    dot_general x1, matrix products, on_device(): jnp.einsum('tmc,ntc->nmc', from_start, grad_conv, precision=full_precision)  58.2 us
    dot_general x1, matrix products, on_device(): jnp.einsum('smc,nmc->nsc', back_rows, end_states, precision=full_precision)  47.3 us
    dot_general x1, matrix products, on_device(): jnp.einsum('tmc,nmc->ntc', into_rows, start_states, precision=full_precis...  46.7 us
  transfers between devices with their start and end apart: 32, of which 30 were waited for; matrix products, arithmetic and copies ran while one was open for 38% of the time, Pallas kernels for 0%

commit v1 on v0

--- a/solution.py
+++ b/solution.py
@@ -12,6 +12,16 @@
     count = lax.axis_size(axis)
     initial, last = (max(0, -steps), min(count, count - steps))
     return lax.ppermute(value, axis, [(source, source + steps) for source in range(initial, last)])
+
+
+def prefix_scan(value, decay_one, axis, direction):
+    count = lax.axis_size(axis)
+    state = passed_along(value, axis, direction)
+    factor, step = decay_one, 1
+    while step < count:
+        state = state + factor * passed_along(state, axis, step * direction)
+        factor, step = factor * factor, step * 2
+    return state
 
 
 def on_device(gated_input, query, out_grad, out_weight, decay_rate, residue):
@@ -50,13 +60,7 @@
     block_states = jnp.einsum("nkmc,kmc->nmc", fwd_coef, block_ends, precision=full_precision)
     local_end = block_states[block_count]
 
-    def relay_forward(hop_index, state_pair):
-        arrived = passed_along(state_pair[1], "ctx", 1)
-        return (arrived, chain_decay * arrived + local_end)
-
-    earlier_state = lax.fori_loop(
-        0, lax.axis_size("ctx") - 1, relay_forward, (zero_state, local_end)
-    )[0]
+    earlier_state = prefix_scan(local_end, chain_decay, "ctx", 1)
     start_states = (
         block_states[:block_count]
         + jnp.exp(-decay_rate[None] * block_rows * block_index[:, None, None]) * earlier_state[None]
@@ -79,13 +83,7 @@
     block_tails = jnp.einsum("nkmc,kmc->nmc", back_coef, block_heads, precision=full_precision)
     local_out = block_tails[0]
 
-    def relay_backward(hop_index, state_pair):
-        arrived = passed_along(state_pair[1], "ctx", -1)
-        return (arrived, chain_decay * arrived + local_out)
-
-    later_state = lax.fori_loop(
-        0, lax.axis_size("ctx") - 1, relay_backward, (zero_state, local_out)
-    )[0]
+    later_state = prefix_scan(local_out, chain_decay, "ctx", -1)
     end_states = (
         block_tails[1:]
         + jnp.exp(-decay_rate[None] * block_rows * (block_count - 1.0 - block_index)[:, None, None])

time: 1080 us -> 797 us (0.74)
  waiting for transfers between devices: 226 us -> 40 us
  starting transfers between devices: 106 us -> 33.6 us
  local copies, waits for them, and re-layouts: 232 us -> 210 us
    ppermute x30 -> x10, waiting for transfers between devices: 225 us -> 38.6 us  [passed_along(): lax.ppermute(value, axis, [(source, source + steps) for source in range(i...]
    ppermute x30 -> x10, starting transfers between devices: 106 us -> 33.6 us  [passed_along(): lax.ppermute(value, axis, [(source, source + steps) for source in range(i...]
    while x60 -> x0, local copies, waits for them, and re-layouts: 19.8 us -> none
  transfers between devices with their start and end apart: 32 -> 12, of which waited for: 30 -> 7; matrix products, arithmetic and copies ran while one was open for 38% -> 67% of each run, Pallas kernels for 0% -> 0%
where the time goes in v1:
time: 797 us; the launch traced here: 786 us
  matrix products  451 us (57%)
  local copies, waits for them, and re-layouts  210 us (26%)
  waiting for transfers between devices  40 us (5%)
  other arithmetic  36.5 us (5%)
  starting transfers between devices  33.6 us (4%)
  between operations  14.6 us (2%)
    gather x2, local copies, waits for them, and re-layouts, on_device(): jnp.take(padded_taps, jnp.asarray(lag_table), axis=0)  149 us
    dot_general x1, matrix products, on_device(): jnp.einsum('tsc,ntc->nsc', toeplitz, grad_conv, precision=full_precision)  120 us
    dot_general x1, matrix products, on_device(): jnp.einsum('tsc,nsc->ntc', toeplitz, input_blocks, precision=full_precision)  111 us
    dot_general x1, matrix products, on_device(): jnp.einsum('tmc,ntc->nmc', from_start, grad_conv, precision=full_precision)  58.2 us
    dot_general x1, matrix products, on_device(): jnp.einsum('smc,nmc->nsc', back_rows, end_states, precision=full_precision)  48.4 us
    dot_general x1, matrix products, on_device(): jnp.einsum('tmc,nmc->ntc', into_rows, start_states, precision=full_precis...  47.6 us
    ppermute x10, waiting for transfers between devices, passed_along(): lax.ppermute(value, axis, [(source, source + steps) for source in range(i...  38.6 us
    dot_general x1, matrix products, on_device(): jnp.einsum('smc,nsc->nmc', to_end, input_blocks, precision=full_precision)  34.5 us
  transfers between devices with their start and end apart: 12, of which 7 were waited for; matrix products, arithmetic and copies ran while one was open for 67% of the time, Pallas kernels for 0%

profile of v1, /device:TPU:23, one launch (start us, length us, event | category | flops | bytes accessed | tf_op | source)
XLA Modules:
  0.0 785.6 jit_solution(485886030296083932)
XLA Ops:
  15.4 34.5 %fusion.24 = f32[16,4096,4]{0,2,1:T(4,128)} fusion(bf16[4,64,4096]{1,0,2:T(4,128)(2,1)} %copy.33, f32[64]{0:T(128)S(1)} %iota_subtract_fusion.3, f32[16,4096]{0,1:T(8,128)} %copy.30), kind=kOutput, calls=%fused_computation.27 | convolution fusion | flops 205520896 | bytes 3408128 | tf_op jit(solution)/shard_map/smc,nsc->nmc/dot_general | solution.py:59
  49.9 6.7 copy.56
  66.1 5.3 collective-permute-start.1
  77.0 26.0 %multiply_reduce_fusion = f32[64,4096]{0,1:T(8,128)} fusion(f32[16,4096]{0,1:T(8,128)} %copy.30, f32[16,4096]{0,1:T(8,128)S(1)} %copy.29), kind=kLoop, calls=%fused_computation.12 | loop fusion | flops 12320768 | bytes 1572864 | tf_op jit(solution)/shard_map/reduce_sum | solution.py:31
  110.5 7.4 collective-permute-done.3
  120.1 33.2 %gather_fusion = f32[4096,4096]{1,0:T(8,128)} fusion(f32[65,4096]{1,0:T(8,128)S(1)} %concatenate.3, s32[4096]{0:T(1024)S(1)} %broadcast_clamp_fusion), kind=kCustom, calls=%fused_computation | custom fusion | bytes 134234112 | tf_op jit(solution)/shard_map/jit(_take)/gather | solution.py:37
  153.3 116.1 %copy.32 = f32[64,64,4096]{1,0,2:T(8,128)} copy(f32[64,64,4096]{2,1,0:T(8,128)} %bitcast.4) | data formatting | bytes 134217728 | tf_op jit(solution)/shard_map/jit(_take)/gather | solution.py:37
  270.8 5.9 copy.35
  276.7 47.6 %fusion.4 = f32[4096,4,64]{2,1,0:T(4,128)} fusion(f32[4,16,4096]{1,0,2:T(4,128)} %copy.35, f32[64]{0:T(128)S(1)} %iota_add_fusion, f32[16,4096]{0,1:T(8,128)} %copy.30, f32[16,4096]{0,1:T(8,128)} %copy-done.9), kind=kOutput, calls=%fused_computation.5 | convolution fusion | flops 209715200 | bytes 5767424 | tf_op jit(solution)/shard_map/tmc,nmc->ntc/dot_general | solution.py:68
  324.3 110.9 %bitcast_add_fusion = f32[4,64,4096]{1,0,2:T(4,128)} fusion(f32[4096,4,64]{2,1,0:T(4,128)} %fusion.4, f32[64,64,4096]{1,0,2:T(8,128)} %copy.32, bf16[4,64,4096]{1,0,2:T(4,128)(2,1)} %copy.33), kind=kOutput, calls=%fused_computation.24 | convolution fusion | flops 806354944 | bytes 77594624 | tf_op jit(solution)/shard_map/tsc,nsc->ntc/dot_general | solution.py:58
  435.2 8.8 %copy.36 = f32[4,64,4096]{2,1,0:T(8,128)} copy(f32[4,64,4096]{1,0,2:T(4,128)} %bitcast_add_fusion) | data formatting | bytes 8388608 | tf_op jit(solution)/shard_map/add | solution.py:69
  444.0 32.2 %convert_multiply_fusion = (f32[256,4096]{1,0:T(8,128)}, bf16[256,4096]{1,0:T(8,128)(2,1)}) fusion(bf16[256,4096]{1,0:T(8,128)(2,1)S(1)} %copy-done.12, f32[4,64,4096]{2,1,0:T(8,128)} %copy.36, bf16[256,8192]{1,0:T(8,128)(2,1)} %all-gather.3.cloned.1.call-done, bf16[4096,8192]{1,0:T(8,128)(2,1)} %all-gather.5.cloned.1.call-done), kind=kOutput, calls=%fused_computation.33 | convolution fusion | flops 17184063488 | bytes 83886080 | tf_op jit(solution)/shard_map/dot_general | solution.py:71
  476.2 8.6 %copy.37 = f32[4,64,4096]{1,0,2:T(4,128)} copy(f32[4,64,4096]{2,1,0:T(8,128)} %bitcast.51) | data formatting | bytes 8388608 | tf_op jit(solution)/shard_map/reshape | solution.py:78
  484.7 58.2 %fusion.23 = f32[16,4096,4]{0,2,1:T(4,128)} fusion(f32[4,64,4096]{1,0,2:T(4,128)} %copy.37, f32[16,4096]{0,1:T(8,128)S(1)} %copy-done.8), kind=kOutput, calls=%fused_computation.26 | convolution fusion | flops 205520896 | bytes 5505024 | tf_op jit(solution)/shard_map/tmc,ntc->nmc/dot_general | solution.py:82
  542.9 6.7 copy.57
  552.9 6.0 collective-permute-start.5
  565.0 6.7 collective-permute-done.6
  574.0 7.9 collective-permute-done.7
  584.9 6.7 collective-permute-done.8
  591.7 5.7 collective-permute-start.9
  597.5 119.6 %fusion.33 = f32[4096,4,64]{2,1,0:T(4,128)} fusion(f32[4,64,4096]{1,0,2:T(4,128)} %copy.37, f32[64,64,4096]{1,0,2:T(8,128)} %copy.32), kind=kOutput, calls=%fused_computation.59 | convolution fusion | flops 805306368 | bytes 75497472 | tf_op jit(solution)/shard_map/tsc,ntc->nsc/dot_general | solution.py:81
  717.4 5.9 copy.40
  723.3 48.4 %fusion.28 = bf16[4,64,4096]{1,0,2:T(4,128)(2,1)} fusion(f32[4096,4,64]{2,1,0:T(4,128)} %fusion.33, f32[4,16,4096]{1,0,2:T(4,128)} %copy.40, f32[64]{0:T(128)S(1)} %iota_subtract_fusion.1, f32[16,4096]{0,1:T(8,128)} %copy.30, f32[16,4096]{0,1:T(8,128)} %copy-done.9), kind=kOutput, calls=%fused_computation.34 | convolution fusion | flops 211812352 | bytes 7864576 | tf_op jit(solution)/shard_map/smc,nmc->nsc/dot_general | solution.py:92
  771.7 6.9 copy.41
  (74 shorter events, 49.2 us)
Async XLA Ops:
  7.2 1.5 copy-start
  7.2 3.5 copy-start.7
  7.2 436.8 %all-gather.3.cloned.1.call-start = ((), (), s32[]{:S(2)}) async-start(), calls=%async_computation | async-start | bytes 6291456 | tf_op jit(solution)/shard_map/all_gather | solution.py:70
  7.9 436.1 %all-gather.5.cloned.1.call-start = ((), (), s32[]{:S(2)}) async-start(), calls=%async_computation.1 | async-start | bytes 71303168 | tf_op jit(solution)/shard_map/all_gather | solution.py:73
  8.7 96.3 %copy-start.2 = (f32[16,4096]{1,0:T(8,128)}, f32[16,4096]{1,0:T(8,128)S(1)}, u32[]{:S(2)}) copy-start(f32[16,4096]{1,0:T(8,128)S(1)} %get-tuple-element.6) | copy-start | bytes 786436
  49.9 21.4 %copy-start.10 = (f32[16,4096]{1,0:T(8,128)S(1)}, f32[16,4096]{1,0:T(8,128)}, u32[]{:S(2)}) copy-start(f32[16,4096]{1,0:T(8,128)} %param.12) | copy-start | bytes 786436
  59.1 7.0 collective-permute-start
  66.1 8.6 %collective-permute-start.1 = (f32[16,4096]{1,0:T(8,128)S(1)}, f32[16,4096]{1,0:T(8,128)S(1)}, u32[]{:S(2)}, u32[]{:S(2)}) collective-permute-start(f32[16,4096]{1,0:T(8,128)S(1)} %collective-permute-done), channel_id=1, source_target_pairs={{0,2},{2,4},{4,6},{6,8},{8,10},{10,12},{12,14},{14,16},{16,18},{18... | collective-permute-start | bytes 786440 | tf_op jit(solution)/shard_map/ppermute | solution.py:14
  72.0 33.0 %copy-start.9 = (f32[16,4096]{0,1:T(8,128)}, f32[16,4096]{0,1:T(8,128)S(1)}, u32[]{:S(2)}) copy-start(f32[16,4096]{0,1:T(8,128)S(1)} %copy.29) | copy-start | bytes 786436
  74.7 28.3 %collective-permute-start.2 = (f32[16,4096]{1,0:T(8,128)S(1)}, f32[16,4096]{1,0:T(8,128)S(1)}, u32[]{:S(2)}, u32[]{:S(2)}) collective-permute-start(f32[16,4096]{1,0:T(8,128)S(1)} %multiply_add_fusion.7), channel_id=1, source_target_pairs={{0,4},{2,6},{4,8},{6,10},{8,12},{10,14},{12,16},{14,18},{16,20},{1... | collective-permute-start | bytes 786440 | tf_op jit(solution)/shard_map/ppermute | solution.py:14
  103.1 17.0 %copy-start.11 = (s32[4096]{0:T(1024)S(1)}, s32[4096]{0:T(1024)}, u32[]{:S(2)}) copy-start(s32[4096]{0:T(1024)} %constant.49) | copy-start | bytes 49156
  103.1 14.8 %collective-permute-start.3 = (f32[16,4096]{1,0:T(8,128)S(1)}, f32[16,4096]{1,0:T(8,128)S(1)}, u32[]{:S(2)}, u32[]{:S(2)}) collective-permute-start(f32[16,4096]{1,0:T(8,128)S(1)} %multiply_add_fusion.6), channel_id=1, source_target_pairs={{0,8},{2,10},{4,12},{6,14},{8,16},{10,18},{12,20},{14,22},{16,24},... | collective-permute-start | bytes 786440 | tf_op jit(solution)/shard_map/ppermute | solution.py:14
  118.6 150.9 %collective-permute-start.4 = (f32[16,4096]{1,0:T(8,128)}, f32[16,4096]{1,0:T(8,128)}, u32[]{:S(2)}, u32[]{:S(2)}) collective-permute-start(f32[16,4096]{1,0:T(8,128)} %multiply_add_fusion.5), channel_id=1, source_target_pairs={{0,16},{2,18},{4,20},{6,22},{8,24},{10,26},{12,28},{14,30},{1,17},... | collective-permute-start | bytes 786440 | tf_op jit(solution)/shard_map/ppermute | solution.py:14
  153.3 116.2 %copy-start.1 = (f32[16,4096]{1,0:T(8,128)S(1)}, f32[16,4096]{1,0:T(8,128)}, u32[]{:S(2)}) copy-start(f32[16,4096]{1,0:T(8,128)} %param.11) | copy-start | bytes 786436
  153.3 117.3 %copy-start.3 = (f32[16,4096]{1,0:T(8,128)S(1)}, f32[16,4096]{1,0:T(8,128)}, u32[]{:S(2)}) copy-start(f32[16,4096]{1,0:T(8,128)} %copy-done.2) | copy-start | bytes 786436
  153.3 117.3 %copy-start.6 = (f32[16,4096,5]{1,0,2:T(8,128)S(1)}, f32[16,4096,5]{1,0,2:T(8,128)}, u32[]{:S(2)}) copy-start(f32[16,4096,5]{1,0,2:T(8,128)} %copy-done.5) | copy-start | bytes 3932164
  435.2 8.8 %copy-start.12 = (bf16[256,4096]{1,0:T(8,128)(2,1)S(1)}, bf16[256,4096]{1,0:T(8,128)(2,1)}, u32[]{:S(2)}) copy-start(bf16[256,4096]{1,0:T(8,128)(2,1)} %param.8) | copy-start | bytes 6291460
  476.1 8.6 %copy-start.8 = (f32[16,4096]{0,1:T(8,128)S(1)}, f32[16,4096]{0,1:T(8,128)}, u32[]{:S(2)}) copy-start(f32[16,4096]{0,1:T(8,128)} %copy.30) | copy-start | bytes 786436
  552.9 10.1 %collective-permute-start.5 = (f32[16,4096]{1,0:T(8,128)S(1)}, f32[16,4096]{1,0:T(8,128)S(1)}, u32[]{:S(2)}, u32[]{:S(2)}) collective-permute-start(f32[16,4096]{1,0:T(8,128)S(1)} %slice_bitcast_fusion), channel_id=1, source_target_pairs={{2,0},{4,2},{6,4},{8,6},{10,8},{12,10},{14,12},{16,14},{18,16},{20... | collective-permute-start | bytes 786440 | tf_op jit(solution)/shard_map/ppermute | solution.py:14
  563.0 8.6 %collective-permute-start.6 = (f32[16,4096]{1,0:T(8,128)S(1)}, f32[16,4096]{1,0:T(8,128)S(1)}, u32[]{:S(2)}, u32[]{:S(2)}) collective-permute-start(f32[16,4096]{1,0:T(8,128)S(1)} %collective-permute-done.5), channel_id=1, source_target_pairs={{2,0},{4,2},{6,4},{8,6},{10,8},{12,10},{14,12},{16,14},{18,16},{20... | collective-permute-start | bytes 786440 | tf_op jit(solution)/shard_map/ppermute | solution.py:14
  571.7 10.2 %collective-permute-start.7 = (f32[16,4096]{1,0:T(8,128)S(1)}, f32[16,4096]{1,0:T(8,128)S(1)}, u32[]{:S(2)}, u32[]{:S(2)}) collective-permute-start(f32[16,4096]{1,0:T(8,128)S(1)} %multiply_add_fusion.3), channel_id=1, source_target_pairs={{4,0},{6,2},{8,4},{10,6},{12,8},{14,10},{16,12},{18,14},{20,16},{2... | collective-permute-start | bytes 786440 | tf_op jit(solution)/shard_map/ppermute | solution.py:14
  581.9 9.7 %collective-permute-start.8 = (f32[16,4096]{1,0:T(8,128)S(1)}, f32[16,4096]{1,0:T(8,128)S(1)}, u32[]{:S(2)}, u32[]{:S(2)}) collective-permute-start(f32[16,4096]{1,0:T(8,128)S(1)} %multiply_add_fusion.2), channel_id=1, source_target_pairs={{8,0},{10,2},{12,4},{14,6},{16,8},{18,10},{20,12},{22,14},{24,16},... | collective-permute-start | bytes 786440 | tf_op jit(solution)/shard_map/ppermute | solution.py:14
  591.7 125.4 %copy-start.4 = (f32[16,4096]{1,0:T(8,128)S(1)}, f32[16,4096]{1,0:T(8,128)}, u32[]{:S(2)}) copy-start(f32[16,4096]{1,0:T(8,128)} %copy-done.2) | copy-start | bytes 786436
  591.7 125.3 %collective-permute-start.9 = (f32[16,4096]{1,0:T(8,128)S(1)}, f32[16,4096]{1,0:T(8,128)S(1)}, u32[]{:S(2)}, u32[]{:S(2)}) collective-permute-start(f32[16,4096]{1,0:T(8,128)S(1)} %multiply_add_fusion.1), channel_id=1, source_target_pairs={{16,0},{18,2},{20,4},{22,6},{24,8},{26,10},{28,12},{30,14},{17,1},... | collective-permute-start | bytes 786440 | tf_op jit(solution)/shard_map/ppermute | solution.py:14
  (1 other events, 1.0 us)
Sparse Core Ops, SparseCore 0:
  9.5 56.6 all-gather.2
  67.8 349.1 all-gather.4

commit v2 on v1

--- a/solution.py
+++ b/solution.py
@@ -5,7 +5,6 @@
 from jax.sharding import PartitionSpec as P
 
 block_rows = 64
-full_precision = lax.Precision.HIGHEST
 
 
 def passed_along(value, axis, steps):
@@ -55,9 +54,9 @@
     chain_decay = jnp.exp(-decay_rate * tok_rows)
     zero_state = jnp.zeros_like(chain_decay)
     input_blocks = gated_input.astype(jnp.float32).reshape(block_count, block_rows, chan_width)
-    local_part = jnp.einsum("tsc,nsc->ntc", toeplitz, input_blocks, precision=full_precision)
-    block_ends = jnp.einsum("smc,nsc->nmc", to_end, input_blocks, precision=full_precision)
-    block_states = jnp.einsum("nkmc,kmc->nmc", fwd_coef, block_ends, precision=full_precision)
+    local_part = jnp.sum(toeplitz[None] * input_blocks[:, None], axis=2)
+    block_ends = jnp.sum(to_end[None] * input_blocks[:, :, None], axis=1)
+    block_states = jnp.sum(fwd_coef * block_ends[None], axis=1)
     local_end = block_states[block_count]
 
     earlier_state = prefix_scan(local_end, chain_decay, "ctx", 1)
@@ -65,7 +64,7 @@
         block_states[:block_count]
         + jnp.exp(-decay_rate[None] * block_rows * block_index[:, None, None]) * earlier_state[None]
     )
-    carried = jnp.einsum("tmc,nmc->ntc", into_rows, start_states, precision=full_precision)
+    carried = jnp.sum(into_rows[None] * start_states[:, None], axis=2)
     conv_out = (local_part + carried).reshape(tok_rows, chan_width)
     grad_rows = lax.all_gather(out_grad, "chan", axis=1, tiled=True)
     grad_mixed = lax.dot_general(
@@ -78,9 +77,9 @@
     grad_conv = (grad_mixed * query.astype(jnp.float32)).reshape(
         block_count, block_rows, chan_width
     )
-    local_back = jnp.einsum("tsc,ntc->nsc", toeplitz, grad_conv, precision=full_precision)
-    block_heads = jnp.einsum("tmc,ntc->nmc", from_start, grad_conv, precision=full_precision)
-    block_tails = jnp.einsum("nkmc,kmc->nmc", back_coef, block_heads, precision=full_precision)
+    local_back = jnp.sum(toeplitz[None] * grad_conv[:, :, None], axis=1)
+    block_heads = jnp.sum(from_start[None] * grad_conv[:, :, None], axis=1)
+    block_tails = jnp.sum(back_coef * block_heads[None], axis=1)
     local_out = block_tails[0]
 
     later_state = prefix_scan(local_out, chain_decay, "ctx", -1)
@@ -89,7 +88,7 @@
         + jnp.exp(-decay_rate[None] * block_rows * (block_count - 1.0 - block_index)[:, None, None])
         * later_state[None]
     )
-    carried_back = jnp.einsum("smc,nmc->nsc", back_rows, end_states, precision=full_precision)
+    carried_back = jnp.sum(back_rows[None] * end_states[:, None], axis=2)
     grad_input = (local_back + carried_back).reshape(tok_rows, chan_width).astype(jnp.bfloat16)
     return (grad_query, grad_input)
 

time: 797 us -> 687 us (0.86)
  matrix products: 451 us -> 31.9 us
  waiting for transfers between devices: 40 us -> 385 us
  local copies, waits for them, and re-layouts: 210 us -> 36 us
  other arithmetic: 36.5 us -> 188 us
  starting transfers between devices: 33.6 us -> 22.9 us
    dot_general x6 -> x0, matrix products: 419 us -> none  [the longest x1 120 us: on_device(): jnp.einsum('tsc,ntc->nsc', toeplitz, grad_conv, precision=full_precision)]
    all_gather x1, waiting for transfers between devices: 0.01 us -> 328 us  [on_device(): lax.all_gather(out_weight, 'ctx', axis=1, tiled=True)]
    gather x2 -> x1, local copies, waits for them, and re-layouts: 149 us -> 33.1 us  [on_device(): jnp.take(padded_taps, jnp.asarray(lag_table), axis=0)]
    reduce_sum x1 -> x5, other arithmetic: 26 us -> 141 us  [the longest x1 79.3 us: on_device(): local_back = jnp.sum(toeplitz[None] * grad_conv[:, :, None], axis=1)]
    mul x0 -> x2, other arithmetic: none -> 29.7 us  [the longest x1 25.6 us: on_device(): residue[None]]
    add x3 -> x0, local copies, waits for them, and re-layouts: 20.6 us -> none  [the longest x1 8.78 us: on_device(): conv_out = (local_part + carried).reshape(tok_rows, chan_width)]
    all_gather x1, waiting for transfers between devices: 0.01 us -> 16.3 us  [on_device(): grad_rows = lax.all_gather(out_grad, 'chan', axis=1, tiled=True)]
    reshape x2 -> x0, local copies, waits for them, and re-layouts: 13.3 us -> none  [the longest x1 8.57 us: on_device(): (grad_mixed * query.astype(jnp.float32)).reshape(block_count, block_rows,...]
  transfers between devices with their start and end apart: 12 -> 12, of which waited for: 7 -> 8; matrix products, arithmetic and copies ran while one was open for 67% -> 23% of each run, Pallas kernels for 0% -> 0%
where the time goes in v2:
time: 687 us; the launch traced here: 678 us
  waiting for transfers between devices  385 us (56%)
  other arithmetic  188 us (27%)
  local copies, waits for them, and re-layouts  36 us (5%)
  matrix products  31.9 us (5%)
  starting transfers between devices  22.9 us (3%)
  between operations  14.4 us (2%)
    all_gather x1, waiting for transfers between devices, on_device(): lax.all_gather(out_weight, 'ctx', axis=1, tiled=True)  328 us
    reduce_sum x1, other arithmetic, on_device(): local_back = jnp.sum(toeplitz[None] * grad_conv[:, :, None], axis=1)  79.3 us
    reduce_sum x1, other arithmetic, on_device(): carried_back = jnp.sum(back_rows[None] * end_states[:, None], axis=2)  42.5 us
    ppermute x10, waiting for transfers between devices, passed_along(): lax.ppermute(value, axis, [(source, source + steps) for source in range(i...  39.3 us
    gather x1, local copies, waits for them, and re-layouts, on_device(): jnp.take(padded_taps, jnp.asarray(lag_table), axis=0)  33.1 us
    dot_general x1, matrix products, on_device(): lax.dot_general(grad_rows, lax.all_gather(out_weight, 'ctx', axis=1, tile...  31.9 us
    mul x1, other arithmetic, on_device(): residue[None]  25.6 us
    ppermute x10, starting transfers between devices, passed_along(): lax.ppermute(value, axis, [(source, source + steps) for source in range(i...  22.9 us
  transfers between devices with their start and end apart: 12, of which 8 were waited for; matrix products, arithmetic and copies ran while one was open for 23% of the time, Pallas kernels for 0%

profile of v2, /device:TPU:23, one launch (start us, length us, event | category | flops | bytes accessed | tf_op | source)
XLA Modules:
  0.0 678.3 jit_solution(10787036393759181768)
XLA Ops:
  8.9 4.1 bitcast_convert_fusion
  13.1 25.6 %exponential_multiply_fusion = (f32[64,16,4096]{2,1,0:T(8,128)}, f32[64,4096]{1,0:T(8,128)}, f32[64,16,4096]{2,1,0:T(8,128)}, f32[64,16,4096]{2,1,0:T(8,128)}, f32[64,16,4096]{2,1,0:T(8,128)}) fusion(f32[64]{0:T(128)S(1)} %iota_subtract_fusion.2, f32[16,4096]{1,0:T(8,128)S(1)} %get-tuple-element.16, f32[16,4096]{1,0:T(8,128)S(1)} %copy-done.12, ...), kind=kLoop, calls=%fused_computation.7 | loop fusion | flops 33292288 | bytes 68682496 | tf_op jit(solution)/shard_map/mul | solution.py:42
  38.6 7.7 %multiply_reduce_fusion.5 = f32[4,16,4096]{2,1,0:T(8,128)S(1)} fusion(f32[4,64,4096]{2,1,0:T(8,128)} %bitcast_convert_fusion, f32[64,16,4096]{2,1,0:T(8,128)} %get-tuple-element.9), kind=kLoop, calls=%fused_computation.6 | loop fusion | flops 33292288 | bytes 22020096 | tf_op jit(solution)/shard_map/reduce_sum | solution.py:58
  46.4 3.5 exponential_select_fusion
  49.9 16.3 %all-gather.3.cloned.1.call-done = bf16[256,8192]{1,0:T(8,128)(2,1)} async-done(((bf16[256,4096]{1,0:T(8,128)(2,1)}), bf16[256,8192]{1,0:T(8,128)(2,1)}) %all-gather.3.cloned.1.call-update) | async-done | bytes 4194320 | tf_op jit(solution)/shard_map/all_gather | solution.py:69
  66.2 328.4 %all-gather.5.cloned.1.call-done = bf16[4096,8192]{1,0:T(8,128)(2,1)} async-done(((bf16[4096,512]{1,0:T(8,128)(2,1)}), bf16[4096,8192]{1,0:T(8,128)(2,1)}) %all-gather.5.cloned.1.call-update) | async-done | bytes 67108880 | tf_op jit(solution)/shard_map/all_gather | solution.py:72
  394.6 31.9 %convert_multiply_fusion = (f32[256,4096]{1,0:T(8,128)}, f32[256,4096]{1,0:T(8,128)}) fusion(bf16[256,4096]{1,0:T(8,128)(2,1)} %param.8, bf16[256,8192]{1,0:T(8,128)(2,1)} %all-gather.3.cloned.1.call-done, bf16[4096,8192]{1,0:T(8,128)(2,1)} %all-gather.5.cloned.1.call-done), kind=kOutput, calls=%fused_computation.18 | convolution fusion | flops 17181966336 | bytes 81788928 | tf_op jit(solution)/shard_map/dot_general | solution.py:70
  426.6 7.7 %multiply_reduce_fusion.3 = f32[4,16,4096]{2,1,0:T(8,128)S(1)} fusion(f32[4,64,4096]{2,1,0:T(8,128)} %bitcast.16, f32[64,16,4096]{2,1,0:T(8,128)} %get-tuple-element.10), kind=kLoop, calls=%fused_computation.4 | loop fusion | flops 33292288 | bytes 22020096 | tf_op jit(solution)/shard_map/reduce_sum | solution.py:81
  434.3 3.4 multiply_reduce_fusion.7
  437.8 2.2 collective-permute-start.5
  439.9 6.4 collective-permute-done.5
  448.3 6.7 collective-permute-done.6
  459.1 6.2 collective-permute-done.7
  465.4 2.2 collective-permute-start.8
  467.6 5.1 collective-permute-start.1
  472.6 2.6 collective-permute-done.8
  475.3 2.2 collective-permute-start.9
  477.5 10.8 %collective-permute-done.9 = f32[16,4096]{1,0:T(8,128)S(1)} collective-permute-done((f32[16,4096]{1,0:T(8,128)S(1)}, f32[16,4096]{1,0:T(8,128)S(1)}, u32[]{:S(2)}, u32[]{:S(2)}) %collective-permute-start.9) | collective-permute-done | bytes 262176 | tf_op jit(solution)/shard_map/ppermute | solution.py:13
  491.2 6.6 collective-permute-done.2
  500.6 33.1 %gather_fusion = f32[4096,4096]{1,0:T(8,128)} fusion(f32[65,4096]{1,0:T(8,128)S(1)} %concatenate.3, s32[4096]{0:T(1024)S(1)} %broadcast_clamp_fusion), kind=kCustom, calls=%fused_computation | custom fusion | bytes 134234112 | tf_op jit(solution)/shard_map/jit(_take)/gather | solution.py:36
  536.2 79.3 %multiply_reduce_fusion = (f32[4,64,4096]{2,1,0:T(8,128)}, f32[4,64,4096]{2,1,0:T(8,128)}) fusion(f32[4,64,4096]{2,1,0:T(8,128)} %bitcast.17, f32[64,64,4096]{2,1,0:T(8,128)} %bitcast, f32[4,64,4096]{2,1,0:T(8,128)} %bitcast_convert_fusion), kind=kLoop, calls=%fused_computation.1 | loop fusion | flops 266338304 | bytes 83886080 | tf_op jit(solution)/shard_map/reduce_sum | solution.py:80
  615.6 2.5 slice_add_fusion
  618.1 42.5 %multiply_reduce_fusion.2 = (f32[4,64,4096]{2,1,0:T(8,128)}, f32[4,64,4096]{2,1,0:T(8,128)}) fusion(f32[4,16,4096]{2,1,0:T(8,128)S(1)} %get-tuple-element.11, f32[64,16,4096]{2,1,0:T(8,128)} %get-tuple-element.4, f32[4,16,4096]{2,1,0:T(8,128)} %get-tuple-element.12, f32[64,16,4096]{2,1,0:T(8,128)} %get-tuple-element.6), kind=kLoop, calls=%fused_computation.3 | loop fusion | flops 65011712 | bytes 44040192 | tf_op jit(solution)/shard_map/reduce_sum | solution.py:91
  660.6 5.4 add_convert_fusion
  (63 shorter events, 21.5 us)
Async XLA Ops:
  7.2 59.0 %all-gather.3.cloned.1.call-start = ((), (), s32[]{:S(2)}) async-start(), calls=%async_computation | async-start | bytes 6291456 | tf_op jit(solution)/shard_map/all_gather | solution.py:69
  7.9 5.2 copy-start.12
  7.9 386.7 %all-gather.5.cloned.1.call-start = ((), (), s32[]{:S(2)}) async-start(), calls=%async_computation.1 | async-start | bytes 71303168 | tf_op jit(solution)/shard_map/all_gather | solution.py:72
  8.9 37.5 %copy-start.9 = (f32[16,4096]{1,0:T(8,128)}, f32[16,4096]{1,0:T(8,128)S(1)}, u32[]{:S(2)}) copy-start(f32[16,4096]{1,0:T(8,128)S(1)} %get-tuple-element.15) | copy-start | bytes 786436
  49.9 407.0 %copy-start.4 = (f32[5,16,4096]{2,1,0:T(8,128)}, f32[5,16,4096]{2,1,0:T(8,128)S(1)}, u32[]{:S(2)}) copy-start(f32[5,16,4096]{2,1,0:T(8,128)S(1)} %get-tuple-element.8) | copy-start | bytes 3932164
  434.3 56.8 %copy-start.7 = (f32[64,4096]{1,0:T(8,128)S(1)}, f32[64,4096]{1,0:T(8,128)}, u32[]{:S(2)}) copy-start(f32[64,4096]{1,0:T(8,128)} %get-tuple-element.5) | copy-start | bytes 3145732
  437.7 62.9 %copy-start.6 = (f32[5,16,4096]{2,1,0:T(8,128)}, f32[5,16,4096]{2,1,0:T(8,128)S(1)}, u32[]{:S(2)}) copy-start(f32[5,16,4096]{2,1,0:T(8,128)S(1)} %multiply_reduce_fusion.7) | copy-start | bytes 3932164
  437.7 62.9 %copy-start.13 = (s32[4096]{0:T(1024)S(1)}, s32[4096]{0:T(1024)}, u32[]{:S(2)}) copy-start(s32[4096]{0:T(1024)} %constant.49) | copy-start | bytes 49156
  437.8 8.6 %collective-permute-start.5 = (f32[16,4096]{1,0:T(8,128)S(1)}, f32[16,4096]{1,0:T(8,128)S(1)}, u32[]{:S(2)}, u32[]{:S(2)}) collective-permute-start(f32[16,4096]{1,0:T(8,128)S(1)} %slice_bitcast_fusion), channel_id=1, source_target_pairs={{2,0},{4,2},{6,4},{8,6},{10,8},{12,10},{14,12},{16,14},{18,16},{20... | collective-permute-start | bytes 786440 | tf_op jit(solution)/shard_map/ppermute | solution.py:13
  446.3 8.6 %collective-permute-start.6 = (f32[16,4096]{1,0:T(8,128)S(1)}, f32[16,4096]{1,0:T(8,128)S(1)}, u32[]{:S(2)}, u32[]{:S(2)}) collective-permute-start(f32[16,4096]{1,0:T(8,128)S(1)} %collective-permute-done.5), channel_id=1, source_target_pairs={{2,0},{4,2},{6,4},{8,6},{10,8},{12,10},{14,12},{16,14},{18,16},{20... | collective-permute-start | bytes 786440 | tf_op jit(solution)/shard_map/ppermute | solution.py:13
  455.0 10.3 %collective-permute-start.7 = (f32[16,4096]{1,0:T(8,128)S(1)}, f32[16,4096]{1,0:T(8,128)S(1)}, u32[]{:S(2)}, u32[]{:S(2)}) collective-permute-start(f32[16,4096]{1,0:T(8,128)S(1)} %multiply_add_fusion.3), channel_id=1, source_target_pairs={{4,0},{6,2},{8,4},{10,6},{12,8},{14,10},{16,12},{18,14},{20,16},{2... | collective-permute-start | bytes 786440 | tf_op jit(solution)/shard_map/ppermute | solution.py:13
  456.9 10.6 %collective-permute-start = (f32[16,4096]{1,0:T(8,128)S(1)}, f32[16,4096]{1,0:T(8,128)S(1)}, u32[]{:S(2)}, u32[]{:S(2)}) collective-permute-start(f32[16,4096]{1,0:T(8,128)S(1)} %slice_bitcast_fusion.1), channel_id=1, source_target_pairs={{0,2},{2,4},{4,6},{6,8},{8,10},{10,12},{12,14},{14,16},{16,18},{18... | collective-permute-start | bytes 786440 | tf_op jit(solution)/shard_map/ppermute | solution.py:13
  465.4 9.9 %collective-permute-start.8 = (f32[16,4096]{1,0:T(8,128)S(1)}, f32[16,4096]{1,0:T(8,128)S(1)}, u32[]{:S(2)}, u32[]{:S(2)}) collective-permute-start(f32[16,4096]{1,0:T(8,128)S(1)} %multiply_add_fusion.2), channel_id=1, source_target_pairs={{8,0},{10,2},{12,4},{14,6},{16,8},{18,10},{20,12},{22,14},{24,16},... | collective-permute-start | bytes 786440 | tf_op jit(solution)/shard_map/ppermute | solution.py:13
  467.6 10.0 %collective-permute-start.1 = (f32[16,4096]{1,0:T(8,128)S(1)}, f32[16,4096]{1,0:T(8,128)S(1)}, u32[]{:S(2)}, u32[]{:S(2)}) collective-permute-start(f32[16,4096]{1,0:T(8,128)S(1)} %collective-permute-done), channel_id=1, source_target_pairs={{0,2},{2,4},{4,6},{6,8},{8,10},{10,12},{12,14},{14,16},{16,18},{18... | collective-permute-start | bytes 786440 | tf_op jit(solution)/shard_map/ppermute | solution.py:13
  475.3 13.0 %collective-permute-start.9 = (f32[16,4096]{1,0:T(8,128)S(1)}, f32[16,4096]{1,0:T(8,128)S(1)}, u32[]{:S(2)}, u32[]{:S(2)}) collective-permute-start(f32[16,4096]{1,0:T(8,128)S(1)} %multiply_add_fusion.1), channel_id=1, source_target_pairs={{16,0},{18,2},{20,4},{22,6},{24,8},{26,10},{28,12},{30,14},{17,1},... | collective-permute-start | bytes 786440 | tf_op jit(solution)/shard_map/ppermute | solution.py:13
  489.1 8.6 %collective-permute-start.2 = (f32[16,4096]{1,0:T(8,128)S(1)}, f32[16,4096]{1,0:T(8,128)S(1)}, u32[]{:S(2)}, u32[]{:S(2)}) collective-permute-start(f32[16,4096]{1,0:T(8,128)S(1)} %get-tuple-element.14), channel_id=1, source_target_pairs={{0,4},{2,6},{4,8},{6,10},{8,12},{10,14},{12,16},{14,18},{16,20},{1... | collective-permute-start | bytes 786440 | tf_op jit(solution)/shard_map/ppermute | solution.py:13
  498.5 35.2 %collective-permute-start.3 = (f32[16,4096]{1,0:T(8,128)}, f32[16,4096]{1,0:T(8,128)}, u32[]{:S(2)}, u32[]{:S(2)}) collective-permute-start(f32[16,4096]{1,0:T(8,128)} %multiply_add_fusion.6), channel_id=1, source_target_pairs={{0,8},{2,10},{4,12},{6,14},{8,16},{10,18},{12,20},{14,22},{16,24},... | collective-permute-start | bytes 786440 | tf_op jit(solution)/shard_map/ppermute | solution.py:13
  500.6 33.1 %copy-start.2 = (f32[16,4096]{1,0:T(8,128)S(1)}, f32[16,4096]{1,0:T(8,128)}, u32[]{:S(2)}) copy-start(f32[16,4096]{1,0:T(8,128)} %param.11) | copy-start | bytes 786436
  534.8 80.6 %collective-permute-start.4 = (f32[16,4096]{1,0:T(8,128)S(1)}, f32[16,4096]{1,0:T(8,128)S(1)}, u32[]{:S(2)}, u32[]{:S(2)}) collective-permute-start(f32[16,4096]{1,0:T(8,128)S(1)} %multiply_add_fusion.5), channel_id=1, source_target_pairs={{0,16},{2,18},{4,20},{6,22},{8,24},{10,26},{12,28},{14,30},{1,17},... | collective-permute-start | bytes 786440 | tf_op jit(solution)/shard_map/ppermute | solution.py:13
  536.1 79.4 %copy-start.5 = (f32[5,16,4096]{2,1,0:T(8,128)S(1)}, f32[5,16,4096]{2,1,0:T(8,128)}, u32[]{:S(2)}) copy-start(f32[5,16,4096]{2,1,0:T(8,128)} %copy-done.4) | copy-start | bytes 3932164
  536.1 79.4 %copy-start.10 = (f32[16,4096]{1,0:T(8,128)S(1)}, f32[16,4096]{1,0:T(8,128)}, u32[]{:S(2)}) copy-start(f32[16,4096]{1,0:T(8,128)} %copy-done.9) | copy-start | bytes 786436
  536.2 79.4 %copy-start.11 = (f32[16,4096]{1,0:T(8,128)S(1)}, f32[16,4096]{1,0:T(8,128)}, u32[]{:S(2)}) copy-start(f32[16,4096]{1,0:T(8,128)} %get-tuple-element.13) | copy-start | bytes 786436
  660.6 5.4 copy-start
  660.6 6.7 copy-start.3
  (2 other events, 3.9 us)
Sparse Core Ops, SparseCore 0:
  9.5 56.6 all-gather.2
  67.7 326.8 all-gather.4

commit v3 on v2

--- a/solution.py
+++ b/solution.py
@@ -4,7 +4,7 @@
 from jax import lax
 from jax.sharding import PartitionSpec as P
 
-block_rows = 64
+block_rows = 32
 
 
 def passed_along(value, axis, steps):

time: 687 us -> 630 us (0.917)
  other arithmetic: 188 us -> 154 us
  local copies, waits for them, and re-layouts: 36 us -> 10.8 us
    reduce_sum x1, other arithmetic: 79.3 us -> 44.6 us  [on_device(): local_back = jnp.sum(toeplitz[None] * grad_conv[:, :, None], axis=1)]
    gather x1, local copies, waits for them, and re-layouts: 33.1 us -> 9.18 us  [on_device(): jnp.take(padded_taps, jnp.asarray(lag_table), axis=0)]
    select_n x1, other arithmetic: 3.49 us -> 14 us  [on_device(): jnp.where((gap_blocks >= 0.0)[:, :, None, None], jnp.exp(-decay_rate[None...]
    mul x1, other arithmetic: 25.6 us -> 15.4 us  [on_device(): residue[None]]
  transfers between devices with their start and end apart: 12 -> 12, of which waited for: 8 -> 8; matrix products, arithmetic and copies ran while one was open for 23% -> 15% of each run, Pallas kernels for 0% -> 0%
where the time goes in v3:
time: 630 us; the launch traced here: 621 us
  waiting for transfers between devices  387 us (61%)
  other arithmetic  154 us (24%)
  matrix products  31.9 us (5%)
  starting transfers between devices  22.9 us (4%)
  between operations  14.3 us (2%)
  local copies, waits for them, and re-layouts  10.8 us (2%)
    all_gather x1, waiting for transfers between devices, on_device(): lax.all_gather(out_weight, 'ctx', axis=1, tiled=True)  328 us
    reduce_sum x1, other arithmetic, on_device(): local_back = jnp.sum(toeplitz[None] * grad_conv[:, :, None], axis=1)  44.6 us
    ppermute x10, waiting for transfers between devices, passed_along(): lax.ppermute(value, axis, [(source, source + steps) for source in range(i...  39.3 us
    reduce_sum x1, other arithmetic, on_device(): carried_back = jnp.sum(back_rows[None] * end_states[:, None], axis=2)  38 us
    dot_general x1, matrix products, on_device(): lax.dot_general(grad_rows, lax.all_gather(out_weight, 'ctx', axis=1, tile...  31.9 us
    ppermute x10, starting transfers between devices, passed_along(): lax.ppermute(value, axis, [(source, source + steps) for source in range(i...  22.8 us
    all_gather x1, waiting for transfers between devices, on_device(): grad_rows = lax.all_gather(out_grad, 'chan', axis=1, tiled=True)  18.1 us
    mul x1, other arithmetic, on_device(): residue[None]  15.4 us
  transfers between devices with their start and end apart: 12, of which 8 were waited for; matrix products, arithmetic and copies ran while one was open for 15% of the time, Pallas kernels for 0%

profile of v3, /device:TPU:23, one launch (start us, length us, event | category | flops | bytes accessed | tf_op | source)
XLA Modules:
  0.0 621.0 jit_solution(6105782716229549417)
XLA Ops:
  8.9 2.4 bitcast_convert_fusion
  11.3 15.4 %exponential_multiply_fusion = (f32[32,16,4096]{2,1,0:T(8,128)}, f32[32,4096]{1,0:T(8,128)}, f32[32,16,4096]{2,1,0:T(8,128)}, f32[32,16,4096]{2,1,0:T(8,128)}, f32[32,16,4096]{2,1,0:T(8,128)}) fusion(f32[32]{0:T(128)S(1)} %iota_subtract_fusion.2, f32[16,4096]{1,0:T(8,128)S(1)} %get-tuple-element.16, f32[16,4096]{1,0:T(8,128)S(1)} %copy-done.8, ...), kind=kLoop, calls=%fused_computation.10 | loop fusion | flops 16646144 | bytes 34603392 | tf_op jit(solution)/shard_map/mul | solution.py:42
  26.7 7.5 %multiply_reduce_fusion.5 = f32[8,16,4096]{2,1,0:T(8,128)} fusion(f32[8,32,4096]{2,1,0:T(8,128)} %bitcast_convert_fusion, f32[32,16,4096]{2,1,0:T(8,128)} %get-tuple-element.9), kind=kLoop, calls=%fused_computation.6 | loop fusion | flops 33030144 | bytes 14680064 | tf_op jit(solution)/shard_map/reduce_sum | solution.py:58
  34.2 14.0 %exponential_select_fusion = (f32[9,8,16,4096]{3,2,1,0:T(8,128)}, f32[9,16,4096]{2,1,0:T(8,128)S(1)}) fusion(f32[9,8]{1,0:T(8,128)S(1)} %fusion.1, f32[16,4096]{1,0:T(8,128)S(1)} %get-tuple-element.15, pred[9,8]{1,0:T(8,128)(4,1)S(1)} %fusion.2, f32[8,16,4096]{2,1,0:T(8,128)} %multiply_reduce_fusion.5), kind=kLoop, calls=%fused_computation.9 | loop fusion | flops 18284544 | bytes 23593320 | tf_op jit(solution)/shard_map/jit(_where)/select_n | solution.py:46
  48.1 18.1 %all-gather.3.cloned.1.call-done = bf16[256,8192]{1,0:T(8,128)(2,1)} async-done(((bf16[256,4096]{1,0:T(8,128)(2,1)}), bf16[256,8192]{1,0:T(8,128)(2,1)}) %all-gather.3.cloned.1.call-update) | async-done | bytes 4194320 | tf_op jit(solution)/shard_map/all_gather | solution.py:69
  66.2 328.4 %all-gather.5.cloned.1.call-done = bf16[4096,8192]{1,0:T(8,128)(2,1)} async-done(((bf16[4096,512]{1,0:T(8,128)(2,1)}), bf16[4096,8192]{1,0:T(8,128)(2,1)}) %all-gather.5.cloned.1.call-update) | async-done | bytes 67108880 | tf_op jit(solution)/shard_map/all_gather | solution.py:72
  394.6 31.9 %convert_multiply_fusion = (f32[256,4096]{1,0:T(8,128)}, f32[256,4096]{1,0:T(8,128)}) fusion(bf16[256,4096]{1,0:T(8,128)(2,1)} %param.8, bf16[256,8192]{1,0:T(8,128)(2,1)} %all-gather.3.cloned.1.call-done, bf16[4096,8192]{1,0:T(8,128)(2,1)} %all-gather.5.cloned.1.call-done), kind=kOutput, calls=%fused_computation.18 | convolution fusion | flops 17181966336 | bytes 81788928 | tf_op jit(solution)/shard_map/dot_general | solution.py:70
  426.5 7.5 %multiply_reduce_fusion.3 = f32[8,16,4096]{2,1,0:T(8,128)} fusion(f32[8,32,4096]{2,1,0:T(8,128)} %bitcast.17, f32[32,16,4096]{2,1,0:T(8,128)} %get-tuple-element.10), kind=kLoop, calls=%fused_computation.4 | loop fusion | flops 33030144 | bytes 14680064 | tf_op jit(solution)/shard_map/reduce_sum | solution.py:81
  434.0 8.0 %multiply_reduce_fusion.6 = f32[9,16,4096]{2,1,0:T(8,128)S(1)} fusion(f32[9,8,16,4096]{3,2,1,0:T(8,128)} %get-tuple-element.7, f32[8,16,4096]{2,1,0:T(8,128)} %multiply_reduce_fusion.3), kind=kLoop, calls=%fused_computation.7 | loop fusion | flops 8847360 | bytes 23330816 | tf_op jit(solution)/shard_map/reduce_sum | solution.py:82
  442.0 2.3 collective-permute-start.5
  444.4 6.4 %collective-permute-done.5 = f32[16,4096]{1,0:T(8,128)S(1)} collective-permute-done((f32[16,4096]{1,0:T(8,128)S(1)}, f32[16,4096]{1,0:T(8,128)S(1)}, u32[]{:S(2)}, u32[]{:S(2)}) %collective-permute-start.5) | collective-permute-done | bytes 262176 | tf_op jit(solution)/shard_map/ppermute | solution.py:13
  452.7 6.7 %collective-permute-done.6 = f32[16,4096]{1,0:T(8,128)S(1)} collective-permute-done((f32[16,4096]{1,0:T(8,128)S(1)}, f32[16,4096]{1,0:T(8,128)S(1)}, u32[]{:S(2)}, u32[]{:S(2)}) %collective-permute-start.6) | collective-permute-done | bytes 262176 | tf_op jit(solution)/shard_map/ppermute | solution.py:13
  463.5 6.2 %collective-permute-done.7 = f32[16,4096]{1,0:T(8,128)S(1)} collective-permute-done((f32[16,4096]{1,0:T(8,128)S(1)}, f32[16,4096]{1,0:T(8,128)S(1)}, u32[]{:S(2)}, u32[]{:S(2)}) %collective-permute-start.7) | collective-permute-done | bytes 262176 | tf_op jit(solution)/shard_map/ppermute | solution.py:13
  469.8 2.2 collective-permute-start.8
  472.0 5.1 collective-permute-start.1
  477.1 2.6 collective-permute-done.8
  479.8 2.2 collective-permute-start.9
  482.0 10.8 %collective-permute-done.9 = f32[16,4096]{1,0:T(8,128)S(1)} collective-permute-done((f32[16,4096]{1,0:T(8,128)S(1)}, f32[16,4096]{1,0:T(8,128)S(1)}, u32[]{:S(2)}, u32[]{:S(2)}) %collective-permute-start.9) | collective-permute-done | bytes 262176 | tf_op jit(solution)/shard_map/ppermute | solution.py:13
  495.6 6.6 %collective-permute-done.2 = f32[16,4096]{1,0:T(8,128)S(1)} collective-permute-done((f32[16,4096]{1,0:T(8,128)S(1)}, f32[16,4096]{1,0:T(8,128)S(1)}, u32[]{:S(2)}, u32[]{:S(2)}) %collective-permute-start.2) | collective-permute-done | bytes 262176 | tf_op jit(solution)/shard_map/ppermute | solution.py:13
  504.9 9.2 %gather_fusion = f32[1024,4096]{1,0:T(8,128)} fusion(f32[33,4096]{1,0:T(8,128)S(1)} %concatenate.3, s32[1024]{0:T(1024)S(1)} %broadcast_clamp_fusion), kind=kCustom, calls=%fused_computation | custom fusion | bytes 33558528 | tf_op jit(solution)/shard_map/jit(_take)/gather | solution.py:36
  516.5 44.6 %multiply_reduce_fusion = (f32[8,32,4096]{2,1,0:T(8,128)}, f32[8,32,4096]{2,1,0:T(8,128)}) fusion(f32[8,32,4096]{2,1,0:T(8,128)} %bitcast.18, f32[32,32,4096]{2,1,0:T(8,128)} %bitcast.16, f32[8,32,4096]{2,1,0:T(8,128)} %bitcast_convert_fusion), kind=kLoop, calls=%fused_computation.1 | loop fusion | flops 132120576 | bytes 33554432 | tf_op jit(solution)/shard_map/reduce_sum | solution.py:80
  562.2 4.3 slice_add_fusion
  566.5 38.0 %multiply_reduce_fusion.2 = (f32[8,32,4096]{2,1,0:T(8,128)}, f32[8,32,4096]{2,1,0:T(8,128)S(1)}) fusion(f32[8,16,4096]{2,1,0:T(8,128)} %get-tuple-element.11, f32[32,16,4096]{2,1,0:T(8,128)} %get-tuple-element.4, f32[8,16,4096]{2,1,0:T(8,128)} %get-tuple-element.12, f32[32,16,4096]{2,1,0:T(8,128)} %get-tuple-element.6), kind=kLoop, calls=%fused_computation.3 | loop fusion | flops 65011712 | bytes 29360128 | tf_op jit(solution)/shard_map/reduce_sum | solution.py:91
  604.5 5.4 add_convert_fusion
  (55 shorter events, 21.0 us)
Async XLA Ops:
  7.2 1.7 copy-start
  7.2 1.8 copy-start.5
  7.2 59.0 %all-gather.3.cloned.1.call-start = ((), (), s32[]{:S(2)}) async-start(), calls=%async_computation | async-start | bytes 6291456 | tf_op jit(solution)/shard_map/all_gather | solution.py:69
  7.9 386.7 %all-gather.5.cloned.1.call-start = ((), (), s32[]{:S(2)}) async-start(), calls=%async_computation.1 | async-start | bytes 71303168 | tf_op jit(solution)/shard_map/all_gather | solution.py:72
  8.7 2.7 copy-start.8
  442.0 53.5 %copy-start.2 = (f32[9,16,4096]{2,1,0:T(8,128)}, f32[9,16,4096]{2,1,0:T(8,128)S(1)}, u32[]{:S(2)}) copy-start(f32[9,16,4096]{2,1,0:T(8,128)S(1)} %multiply_reduce_fusion.6) | copy-start | bytes 7077892
  442.0 53.5 %copy-start.4 = (f32[32,4096]{1,0:T(8,128)S(1)}, f32[32,4096]{1,0:T(8,128)}, u32[]{:S(2)}) copy-start(f32[32,4096]{1,0:T(8,128)} %get-tuple-element.5) | copy-start | bytes 1572868
  442.0 62.8 %copy-start.9 = (s32[1024]{0:T(1024)S(1)}, s32[1024]{0:T(1024)}, u32[]{:S(2)}) copy-start(s32[1024]{0:T(1024)} %constant.49) | copy-start | bytes 12292
  442.0 8.7 %collective-permute-start.5 = (f32[16,4096]{1,0:T(8,128)S(1)}, f32[16,4096]{1,0:T(8,128)S(1)}, u32[]{:S(2)}, u32[]{:S(2)}) collective-permute-start(f32[16,4096]{1,0:T(8,128)S(1)} %slice_bitcast_fusion), channel_id=1, source_target_pairs={{2,0},{4,2},{6,4},{8,6},{10,8},{12,10},{14,12},{16,14},{18,16},{20... | collective-permute-start | bytes 786440 | tf_op jit(solution)/shard_map/ppermute | solution.py:13
  450.8 8.6 %collective-permute-start.6 = (f32[16,4096]{1,0:T(8,128)S(1)}, f32[16,4096]{1,0:T(8,128)S(1)}, u32[]{:S(2)}, u32[]{:S(2)}) collective-permute-start(f32[16,4096]{1,0:T(8,128)S(1)} %collective-permute-done.5), channel_id=1, source_target_pairs={{2,0},{4,2},{6,4},{8,6},{10,8},{12,10},{14,12},{16,14},{18,16},{20... | collective-permute-start | bytes 786440 | tf_op jit(solution)/shard_map/ppermute | solution.py:13
  459.4 10.3 %collective-permute-start.7 = (f32[16,4096]{1,0:T(8,128)S(1)}, f32[16,4096]{1,0:T(8,128)S(1)}, u32[]{:S(2)}, u32[]{:S(2)}) collective-permute-start(f32[16,4096]{1,0:T(8,128)S(1)} %multiply_add_fusion.3), channel_id=1, source_target_pairs={{4,0},{6,2},{8,4},{10,6},{12,8},{14,10},{16,12},{18,14},{20,16},{2... | collective-permute-start | bytes 786440 | tf_op jit(solution)/shard_map/ppermute | solution.py:13
  461.4 10.6 %collective-permute-start = (f32[16,4096]{1,0:T(8,128)S(1)}, f32[16,4096]{1,0:T(8,128)S(1)}, u32[]{:S(2)}, u32[]{:S(2)}) collective-permute-start(f32[16,4096]{1,0:T(8,128)S(1)} %slice_bitcast_fusion.1), channel_id=1, source_target_pairs={{0,2},{2,4},{4,6},{6,8},{8,10},{10,12},{12,14},{14,16},{16,18},{18... | collective-permute-start | bytes 786440 | tf_op jit(solution)/shard_map/ppermute | solution.py:13
  469.8 9.9 %collective-permute-start.8 = (f32[16,4096]{1,0:T(8,128)S(1)}, f32[16,4096]{1,0:T(8,128)S(1)}, u32[]{:S(2)}, u32[]{:S(2)}) collective-permute-start(f32[16,4096]{1,0:T(8,128)S(1)} %multiply_add_fusion.2), channel_id=1, source_target_pairs={{8,0},{10,2},{12,4},{14,6},{16,8},{18,10},{20,12},{22,14},{24,16},... | collective-permute-start | bytes 786440 | tf_op jit(solution)/shard_map/ppermute | solution.py:13
  472.0 10.0 %collective-permute-start.1 = (f32[16,4096]{1,0:T(8,128)S(1)}, f32[16,4096]{1,0:T(8,128)S(1)}, u32[]{:S(2)}, u32[]{:S(2)}) collective-permute-start(f32[16,4096]{1,0:T(8,128)S(1)} %collective-permute-done), channel_id=1, source_target_pairs={{0,2},{2,4},{4,6},{6,8},{8,10},{10,12},{12,14},{14,16},{16,18},{18... | collective-permute-start | bytes 786440 | tf_op jit(solution)/shard_map/ppermute | solution.py:13
  479.8 13.0 %collective-permute-start.9 = (f32[16,4096]{1,0:T(8,128)S(1)}, f32[16,4096]{1,0:T(8,128)S(1)}, u32[]{:S(2)}, u32[]{:S(2)}) collective-permute-start(f32[16,4096]{1,0:T(8,128)S(1)} %multiply_add_fusion.1), channel_id=1, source_target_pairs={{16,0},{18,2},{20,4},{22,6},{24,8},{26,10},{28,12},{30,14},{17,1},... | collective-permute-start | bytes 786440 | tf_op jit(solution)/shard_map/ppermute | solution.py:13
  493.6 8.6 %collective-permute-start.2 = (f32[16,4096]{1,0:T(8,128)S(1)}, f32[16,4096]{1,0:T(8,128)S(1)}, u32[]{:S(2)}, u32[]{:S(2)}) collective-permute-start(f32[16,4096]{1,0:T(8,128)S(1)} %get-tuple-element.14), channel_id=1, source_target_pairs={{0,4},{2,6},{4,8},{6,10},{8,12},{10,14},{12,16},{14,18},{16,20},{1... | collective-permute-start | bytes 786440 | tf_op jit(solution)/shard_map/ppermute | solution.py:13
  502.9 11.1 %collective-permute-start.3 = (f32[16,4096]{1,0:T(8,128)}, f32[16,4096]{1,0:T(8,128)}, u32[]{:S(2)}, u32[]{:S(2)}) collective-permute-start(f32[16,4096]{1,0:T(8,128)} %multiply_add_fusion.6), channel_id=1, source_target_pairs={{0,8},{2,10},{4,12},{6,14},{8,16},{10,18},{12,20},{14,22},{16,24},... | collective-permute-start | bytes 786440 | tf_op jit(solution)/shard_map/ppermute | solution.py:13
  515.2 45.9 %copy-start.7 = (f32[16,4096]{1,0:T(8,128)}, f32[16,4096]{1,0:T(8,128)S(1)}, u32[]{:S(2)}) copy-start(f32[16,4096]{1,0:T(8,128)S(1)} %multiply_add_fusion.5) | copy-start | bytes 786436
  515.2 45.9 %collective-permute-start.4 = (f32[16,4096]{1,0:T(8,128)S(1)}, f32[16,4096]{1,0:T(8,128)}, u32[]{:S(2)}, u32[]{:S(2)}) collective-permute-start(f32[16,4096]{1,0:T(8,128)S(1)} %multiply_add_fusion.5), channel_id=1, source_target_pairs={{0,16},{2,18},{4,20},{6,22},{8,24},{10,26},{12,28},{14,30},{1,17},... | collective-permute-start | bytes 786440 | tf_op jit(solution)/shard_map/ppermute | solution.py:13
  516.5 45.7 %copy-start.6 = (f32[16,4096]{1,0:T(8,128)S(1)}, f32[16,4096]{1,0:T(8,128)}, u32[]{:S(2)}) copy-start(f32[16,4096]{1,0:T(8,128)} %get-tuple-element.13) | copy-start | bytes 786436
  604.5 5.4 copy-start.1
  610.0 2.2 copy-start.3
Sparse Core Ops, SparseCore 0:
  9.5 56.6 all-gather.2
  67.8 326.8 all-gather.4

commit v4 on v3

--- a/solution.py
+++ b/solution.py
@@ -4,7 +4,7 @@
 from jax import lax
 from jax.sharding import PartitionSpec as P
 
-block_rows = 32
+block_rows = 16
 
 
 def passed_along(value, axis, steps):

time: 630 us -> 673 us (1.068)
  waiting for transfers between devices: 387 us -> 426 us
  other arithmetic: 154 us -> 161 us
    reduce_sum x2 -> x0, other arithmetic: 52.1 us -> none  [the longest x1 44.6 us: on_device(): local_back = jnp.sum(toeplitz[None] * grad_conv[:, :, None], axis=1)]
    reduce_sum x1, other arithmetic: 7.47 us -> 42.8 us  [on_device(): block_heads = jnp.sum(from_start[None] * grad_conv[:, :, None], axis=1)]
    all_gather x1, waiting for transfers between devices: 18.1 us -> 43.7 us  [on_device(): grad_rows = lax.all_gather(out_grad, 'chan', axis=1, tiled=True)]
    reduce_sum x1, other arithmetic: 7.97 us -> 26.4 us  [on_device(): block_tails = jnp.sum(back_coef * block_heads[None], axis=1)]
    select_n x1, other arithmetic: 14 us -> 27.6 us  [on_device(): jnp.where((gap_blocks >= 0.0)[:, :, None, None], jnp.exp(-decay_rate[None...]
    ppermute x10, waiting for transfers between devices: 39.3 us -> 51.9 us  [passed_along(): lax.ppermute(value, axis, [(source, source + steps) for source in range(i...]
    mul x1, other arithmetic: 15.4 us -> 6.9 us  [on_device(): residue[None]]
  transfers between devices with their start and end apart: 12 -> 12, of which waited for: 8 -> 10; matrix products, arithmetic and copies ran while one was open for 15% -> 2% of each run, Pallas kernels for 0% -> 0%
where the time goes in v4:
time: 673 us; the launch traced here: 663 us
  waiting for transfers between devices  426 us (63%)
  other arithmetic  161 us (24%)
  matrix products  31.9 us (5%)
  starting transfers between devices  23 us (3%)
  between operations  14.3 us (2%)
  local copies, waits for them, and re-layouts  7.83 us (1%)
    all_gather x1, waiting for transfers between devices, on_device(): lax.all_gather(out_weight, 'ctx', axis=1, tiled=True)  328 us
    ppermute x10, waiting for transfers between devices, passed_along(): lax.ppermute(value, axis, [(source, source + steps) for source in range(i...  51.9 us
    all_gather x1, waiting for transfers between devices, on_device(): grad_rows = lax.all_gather(out_grad, 'chan', axis=1, tiled=True)  43.7 us
    reduce_sum x1, other arithmetic, on_device(): block_heads = jnp.sum(from_start[None] * grad_conv[:, :, None], axis=1)  42.8 us
    reduce_sum x1, other arithmetic, on_device(): carried_back = jnp.sum(back_rows[None] * end_states[:, None], axis=2)  42.6 us
    dot_general x1, matrix products, on_device(): lax.dot_general(grad_rows, lax.all_gather(out_weight, 'ctx', axis=1, tile...  31.9 us
    select_n x1, other arithmetic, on_device(): jnp.where((gap_blocks >= 0.0)[:, :, None, None], jnp.exp(-decay_rate[None...  27.6 us
    reduce_sum x1, other arithmetic, on_device(): block_tails = jnp.sum(back_coef * block_heads[None], axis=1)  26.4 us
  transfers between devices with their start and end apart: 12, of which 10 were waited for; matrix products, arithmetic and copies ran while one was open for 2% of the time, Pallas kernels for 0%

profile of v4, /device:TPU:23, one launch (start us, length us, event | category | flops | bytes accessed | tf_op | source)
XLA Modules:
  0.0 663.1 jit_solution(8083075626741920008)
XLA Ops:
  8.8 6.9 %exponential_multiply_fusion = (f32[16,16,4096]{2,1,0:T(8,128)}, f32[16,4096]{1,0:T(8,128)S(1)}, f32[16,16,4096]{2,1,0:T(8,128)}, f32[16,16,4096]{2,1,0:T(8,128)}, f32[16,16,4096]{2,1,0:T(8,128)}) fusion(f32[16]{0:T(128)S(1)} %iota_subtract_fusion.1, f32[16,4096]{1,0:T(8,128)S(1)} %get-tuple-element.18, f32[16,4096]{1,0:T(8,128)S(1)} %copy-done.8, ...), kind=kLoop, calls=%fused_computation.15 | loop fusion | flops 8323072 | bytes 17563840 | tf_op jit(solution)/shard_map/mul | solution.py:42
  15.7 4.0 gather_fusion
  19.9 2.6 bitcast_convert_fusion
  22.5 43.7 %all-gather.3.cloned.1.call-done = bf16[256,8192]{1,0:T(8,128)(2,1)} async-done(((bf16[256,4096]{1,0:T(8,128)(2,1)}), bf16[256,8192]{1,0:T(8,128)(2,1)}) %all-gather.3.cloned.1.call-update) | async-done | bytes 4194320 | tf_op jit(solution)/shard_map/all_gather | solution.py:69
  66.2 328.5 %all-gather.5.cloned.1.call-done = bf16[4096,8192]{1,0:T(8,128)(2,1)} async-done(((bf16[4096,512]{1,0:T(8,128)(2,1)}), bf16[4096,8192]{1,0:T(8,128)(2,1)}) %all-gather.5.cloned.1.call-update) | async-done | bytes 67108880 | tf_op jit(solution)/shard_map/all_gather | solution.py:72
  394.7 31.9 %convert_multiply_fusion = (f32[256,4096]{1,0:T(8,128)}, f32[256,4096]{1,0:T(8,128)}) fusion(bf16[256,4096]{1,0:T(8,128)(2,1)} %param.8, bf16[256,8192]{1,0:T(8,128)(2,1)} %all-gather.3.cloned.1.call-done, bf16[4096,8192]{1,0:T(8,128)(2,1)} %all-gather.5.cloned.1.call-done), kind=kOutput, calls=%fused_computation.16 | convolution fusion | flops 17181966336 | bytes 81788928 | tf_op jit(solution)/shard_map/dot_general | solution.py:70
  426.6 42.8 %multiply_reduce_fusion.3 = (f32[16,16,4096]{2,1,0:T(8,128)}, f32[16,16,4096]{2,1,0:T(8,128)}, f32[16,16,4096]{2,1,0:T(8,128)}, f32[16,16,4096]{2,1,0:T(8,128)}) fusion(f32[16,16,4096]{2,1,0:T(8,128)} %get-tuple-element.12, f32[16,16,4096]{2,1,0:T(8,128)} %bitcast.17, f32[16,16,4096]{2,1,0:T(8,128)} %bitcast.16, f32[16,16,4096]{2,1,0:T(8,128)} %bitcast_convert_fusion, ...), kind=kLoop, calls=%fused_computation.5 | loop fusion | flops 130023424 | bytes 37748736 | tf_op jit(solution)/shard_map/reduce_sum | solution.py:81
  469.4 27.6 %exponential_select_fusion = (f32[17,16,16,4096]{3,2,1,0:T(8,128)}, f32[17,16,4096]{2,1,0:T(8,128)}) fusion(f32[17,16]{1,0:T(8,128)S(1)} %fusion.1, f32[16,4096]{1,0:T(8,128)S(1)} %get-tuple-element.17, pred[17,16]{1,0:T(8,128)(4,1)S(1)} %fusion.2, f32[16,16,4096]{2,1,0:T(8,128)} %get-tuple-element.5), kind=kLoop, calls=%fused_computation.3 | loop fusion | flops 70189056 | bytes 80217424 | tf_op jit(solution)/shard_map/jit(_where)/select_n | solution.py:46
  497.0 26.4 %multiply_reduce_fusion = f32[17,16,4096]{2,1,0:T(8,128)} fusion(f32[17,16,16,4096]{3,2,1,0:T(8,128)} %get-tuple-element.9, f32[16,16,4096]{2,1,0:T(8,128)} %get-tuple-element.2), kind=kLoop, calls=%fused_computation.1 | loop fusion | flops 34537472 | bytes 79953920 | tf_op jit(solution)/shard_map/reduce_sum | solution.py:82
  524.4 2.4 collective-permute-start.5
  526.9 6.4 collective-permute-done.5
  535.2 6.7 %collective-permute-done.6 = f32[16,4096]{1,0:T(8,128)S(1)} collective-permute-done((f32[16,4096]{1,0:T(8,128)S(1)}, f32[16,4096]{1,0:T(8,128)S(1)}, u32[]{:S(2)}, u32[]{:S(2)}) %collective-permute-start.6) | collective-permute-done | bytes 262176 | tf_op jit(solution)/shard_map/ppermute | solution.py:13
  546.0 6.2 collective-permute-done.7
  552.3 2.2 collective-permute-start.8
  554.5 5.1 collective-permute-start.1
  559.6 2.6 collective-permute-done.8
  562.3 2.2 collective-permute-start.9
  564.5 10.8 %collective-permute-done.9 = f32[16,4096]{1,0:T(8,128)S(1)} collective-permute-done((f32[16,4096]{1,0:T(8,128)S(1)}, f32[16,4096]{1,0:T(8,128)S(1)}, u32[]{:S(2)}, u32[]{:S(2)}) %collective-permute-start.9) | collective-permute-done | bytes 262176 | tf_op jit(solution)/shard_map/ppermute | solution.py:13
  577.4 6.7 %collective-permute-done.2 = f32[16,4096]{1,0:T(8,128)S(1)} collective-permute-done((f32[16,4096]{1,0:T(8,128)S(1)}, f32[16,4096]{1,0:T(8,128)S(1)}, u32[]{:S(2)}, u32[]{:S(2)}) %collective-permute-start.2) | collective-permute-done | bytes 262176 | tf_op jit(solution)/shard_map/ppermute | solution.py:13
  586.0 5.7 collective-permute-done.3
  593.1 6.8 %collective-permute-done.4 = f32[16,4096]{1,0:T(8,128)S(1)} collective-permute-done((f32[16,4096]{1,0:T(8,128)S(1)}, f32[16,4096]{1,0:T(8,128)S(1)}, u32[]{:S(2)}, u32[]{:S(2)}) %collective-permute-start.4) | collective-permute-done | bytes 262176 | tf_op jit(solution)/shard_map/ppermute | solution.py:13
  600.1 3.9 slice_add_fusion
  604.0 42.6 %multiply_reduce_fusion.2 = (f32[16,16,4096]{2,1,0:T(8,128)}, f32[16,16,4096]{2,1,0:T(8,128)}) fusion(f32[16,16,4096]{2,1,0:T(8,128)} %get-tuple-element.13, f32[16,16,4096]{2,1,0:T(8,128)} %get-tuple-element.6, f32[16,16,4096]{2,1,0:T(8,128)} %get-tuple-element.14, f32[16,16,4096]{2,1,0:T(8,128)} %get-tuple-element.8), kind=kLoop, calls=%fused_computation.4 | loop fusion | flops 65011712 | bytes 25165824 | tf_op jit(solution)/shard_map/reduce_sum | solution.py:91
  646.6 4.2 add_convert_fusion
  (52 shorter events, 19.8 us)
Async XLA Ops:
  7.2 1.5 copy-start.5
  7.2 1.6 copy-start.8
  7.2 59.0 %all-gather.3.cloned.1.call-start = ((), (), s32[]{:S(2)}) async-start(), calls=%async_computation | async-start | bytes 6291456 | tf_op jit(solution)/shard_map/all_gather | solution.py:69
  7.9 386.8 %all-gather.5.cloned.1.call-start = ((), (), s32[]{:S(2)}) async-start(), calls=%async_computation.1 | async-start | bytes 71303168 | tf_op jit(solution)/shard_map/all_gather | solution.py:72
  8.8 6.9 %copy-start.9 = (s32[256]{0:T(256)S(1)}, s32[256]{0:T(256)}, u32[]{:S(2)}) copy-start(s32[256]{0:T(256)} %constant.47) | copy-start | bytes 3076
  15.7 4.2 copy-start.7
  497.0 46.8 %copy-start = (f32[17,16,4096]{2,1,0:T(8,128)S(1)}, f32[17,16,4096]{2,1,0:T(8,128)}, u32[]{:S(2)}) copy-start(f32[17,16,4096]{2,1,0:T(8,128)} %get-tuple-element.10) | copy-start | bytes 13369348
  524.4 75.6 %copy-start.1 = (f32[17,16,4096]{2,1,0:T(8,128)S(1)}, f32[17,16,4096]{2,1,0:T(8,128)}, u32[]{:S(2)}) copy-start(f32[17,16,4096]{2,1,0:T(8,128)} %multiply_reduce_fusion) | copy-start | bytes 13369348
  524.4 8.9 %collective-permute-start.5 = (f32[16,4096]{1,0:T(8,128)S(1)}, f32[16,4096]{1,0:T(8,128)S(1)}, u32[]{:S(2)}, u32[]{:S(2)}) collective-permute-start(f32[16,4096]{1,0:T(8,128)S(1)} %slice_bitcast_fusion), channel_id=1, source_target_pairs={{2,0},{4,2},{6,4},{8,6},{10,8},{12,10},{14,12},{16,14},{18,16},{20... | collective-permute-start | bytes 786440 | tf_op jit(solution)/shard_map/ppermute | solution.py:13
  533.3 8.6 %collective-permute-start.6 = (f32[16,4096]{1,0:T(8,128)S(1)}, f32[16,4096]{1,0:T(8,128)S(1)}, u32[]{:S(2)}, u32[]{:S(2)}) collective-permute-start(f32[16,4096]{1,0:T(8,128)S(1)} %collective-permute-done.5), channel_id=1, source_target_pairs={{2,0},{4,2},{6,4},{8,6},{10,8},{12,10},{14,12},{16,14},{18,16},{20... | collective-permute-start | bytes 786440 | tf_op jit(solution)/shard_map/ppermute | solution.py:13
  541.9 10.3 %collective-permute-start.7 = (f32[16,4096]{1,0:T(8,128)S(1)}, f32[16,4096]{1,0:T(8,128)S(1)}, u32[]{:S(2)}, u32[]{:S(2)}) collective-permute-start(f32[16,4096]{1,0:T(8,128)S(1)} %multiply_add_fusion.3), channel_id=1, source_target_pairs={{4,0},{6,2},{8,4},{10,6},{12,8},{14,10},{16,12},{18,14},{20,16},{2... | collective-permute-start | bytes 786440 | tf_op jit(solution)/shard_map/ppermute | solution.py:13
  543.9 10.6 %collective-permute-start = (f32[16,4096]{1,0:T(8,128)S(1)}, f32[16,4096]{1,0:T(8,128)S(1)}, u32[]{:S(2)}, u32[]{:S(2)}) collective-permute-start(f32[16,4096]{1,0:T(8,128)S(1)} %slice_bitcast_fusion.1), channel_id=1, source_target_pairs={{0,2},{2,4},{4,6},{6,8},{8,10},{10,12},{12,14},{14,16},{16,18},{18... | collective-permute-start | bytes 786440 | tf_op jit(solution)/shard_map/ppermute | solution.py:13
  552.3 9.9 %collective-permute-start.8 = (f32[16,4096]{1,0:T(8,128)S(1)}, f32[16,4096]{1,0:T(8,128)S(1)}, u32[]{:S(2)}, u32[]{:S(2)}) collective-permute-start(f32[16,4096]{1,0:T(8,128)S(1)} %multiply_add_fusion.2), channel_id=1, source_target_pairs={{8,0},{10,2},{12,4},{14,6},{16,8},{18,10},{20,12},{22,14},{24,16},... | collective-permute-start | bytes 786440 | tf_op jit(solution)/shard_map/ppermute | solution.py:13
  554.5 10.0 %collective-permute-start.1 = (f32[16,4096]{1,0:T(8,128)S(1)}, f32[16,4096]{1,0:T(8,128)S(1)}, u32[]{:S(2)}, u32[]{:S(2)}) collective-permute-start(f32[16,4096]{1,0:T(8,128)S(1)} %collective-permute-done), channel_id=1, source_target_pairs={{0,2},{2,4},{4,6},{6,8},{8,10},{10,12},{12,14},{14,16},{16,18},{18... | collective-permute-start | bytes 786440 | tf_op jit(solution)/shard_map/ppermute | solution.py:13
  562.3 13.0 %collective-permute-start.9 = (f32[16,4096]{1,0:T(8,128)S(1)}, f32[16,4096]{1,0:T(8,128)S(1)}, u32[]{:S(2)}, u32[]{:S(2)}) collective-permute-start(f32[16,4096]{1,0:T(8,128)S(1)} %multiply_add_fusion.1), channel_id=1, source_target_pairs={{16,0},{18,2},{20,4},{22,6},{24,8},{26,10},{28,12},{30,14},{17,1},... | collective-permute-start | bytes 786440 | tf_op jit(solution)/shard_map/ppermute | solution.py:13
  575.4 8.6 %collective-permute-start.2 = (f32[16,4096]{1,0:T(8,128)S(1)}, f32[16,4096]{1,0:T(8,128)S(1)}, u32[]{:S(2)}, u32[]{:S(2)}) collective-permute-start(f32[16,4096]{1,0:T(8,128)S(1)} %get-tuple-element.16), channel_id=1, source_target_pairs={{0,4},{2,6},{4,8},{6,10},{8,12},{10,14},{12,16},{14,18},{16,20},{1... | collective-permute-start | bytes 786440 | tf_op jit(solution)/shard_map/ppermute | solution.py:13
  584.1 7.7 %collective-permute-start.3 = (f32[16,4096]{1,0:T(8,128)S(1)}, f32[16,4096]{1,0:T(8,128)S(1)}, u32[]{:S(2)}, u32[]{:S(2)}) collective-permute-start(f32[16,4096]{1,0:T(8,128)S(1)} %multiply_add_fusion.6), channel_id=1, source_target_pairs={{0,8},{2,10},{4,12},{6,14},{8,16},{10,18},{12,20},{14,22},{16,24},... | collective-permute-start | bytes 786440 | tf_op jit(solution)/shard_map/ppermute | solution.py:13
  591.8 8.1 %collective-permute-start.4 = (f32[16,4096]{1,0:T(8,128)S(1)}, f32[16,4096]{1,0:T(8,128)S(1)}, u32[]{:S(2)}, u32[]{:S(2)}) collective-permute-start(f32[16,4096]{1,0:T(8,128)S(1)} %multiply_add_fusion.5), channel_id=1, source_target_pairs={{0,16},{2,18},{4,20},{6,22},{8,24},{10,26},{12,28},{14,30},{1,17},... | collective-permute-start | bytes 786440 | tf_op jit(solution)/shard_map/ppermute | solution.py:13
  604.0 42.6 %copy-start.3 = (f32[16,16,4096]{2,1,0:T(8,128)S(1)}, f32[16,16,4096]{2,1,0:T(8,128)}, u32[]{:S(2)}) copy-start(f32[16,16,4096]{2,1,0:T(8,128)} %get-tuple-element.3) | copy-start | bytes 12582916
  646.6 4.2 copy-start.2
  646.6 5.5 copy-start.4
  652.1 2.2 copy-start.6
Sparse Core Ops, SparseCore 0:
  9.5 56.6 all-gather.2
  67.8 326.8 all-gather.4
